TPU v7x, 32 devices: a whole 2x2x4 slice. The times are simulated.
32 devices in a mesh: fsdp: 4 (over x, core), ctx: 2 (over y), tensor: 4 (over z).
Axes of the slice: x: 2, y: 2, z: 4, core: 2. Of those that a mesh axis runs over, the one named last changes fastest.
Arguments:
- frames_in: bfloat16 [16, 1024, 768], P('fsdp', ('ctx', 'tensor')), may hold values from -6 to 6
- out_cotangent: bfloat16 [16, 1024, 768], P('fsdp', ('ctx', 'tensor')), may hold values from -6 to 6
- attend_weight: float32 [3, 768, 768], P(None, ('fsdp', 'ctx'), 'tensor'), as said below
- output_weight: float32 [768, 768], P('tensor', ('fsdp', 'ctx')), may hold values from -0.875 to 0.875
- up_weight: float32 [768, 3072], P(('fsdp', 'ctx'), 'tensor'), may hold values from -0.21875 to 0.21875
- down_weight: float32 [3072, 768], P('tensor', ('fsdp', 'ctx')), may hold values from -0.109375 to 0.109375
- vectors: float32 [12, 768], replicated, as said below
- attend_mean: float32 [3, 768, 768], P(None, ('fsdp', 'ctx'), 'tensor'), may hold values from -24 to 24
- attend_square: float32 [3, 768, 768], P(None, ('fsdp', 'ctx'), 'tensor'), may hold values from 0.32768 to 1.6384
- output_mean: float32 [768, 768], P('tensor', ('fsdp', 'ctx')), may hold values from -24 to 24
- output_square: float32 [768, 768], P('tensor', ('fsdp', 'ctx')), may hold values from 0.32768 to 1.6384
- up_mean: float32 [768, 3072], P(('fsdp', 'ctx'), 'tensor'), may hold values from -24 to 24
- up_square: float32 [768, 3072], P(('fsdp', 'ctx'), 'tensor'), may hold values from 0.32768 to 1.6384
- down_mean: float32 [3072, 768], P('tensor', ('fsdp', 'ctx')), may hold values from -24 to 24
- down_square: float32 [3072, 768], P('tensor', ('fsdp', 'ctx')), may hold values from 0.32768 to 1.6384
- vector_mean: float32 [12, 768], replicated, may hold values from -80 to 80
- vector_square: float32 [12, 768], replicated, may hold values from 3.2768 to 32.768
Outputs:
- frames_out: bfloat16 [16, 1024, 768], P('fsdp', ('ctx', 'tensor'))
- frames_grad: float32 [16, 1024, 768], P('fsdp', ('ctx', 'tensor'))
- attend_grad: float32 [3, 768, 768], P(None, ('fsdp', 'ctx'), 'tensor')
- output_grad: float32 [768, 768], P('tensor', ('fsdp', 'ctx'))
- up_grad: float32 [768, 3072], P(('fsdp', 'ctx'), 'tensor')
- down_grad: float32 [3072, 768], P('tensor', ('fsdp', 'ctx'))
- vector_grad: float32 [12, 768], replicated
- attend_new: float32 [3, 768, 768], P(None, ('fsdp', 'ctx'), 'tensor')
- output_new: float32 [768, 768], P('tensor', ('fsdp', 'ctx'))
- up_new: float32 [768, 3072], P(('fsdp', 'ctx'), 'tensor')
- down_new: float32 [3072, 768], P('tensor', ('fsdp', 'ctx'))
- vector_new: float32 [12, 768], replicated
- attend_mean_new: float32 [3, 768, 768], P(None, ('fsdp', 'ctx'), 'tensor')
- attend_square_new: float32 [3, 768, 768], P(None, ('fsdp', 'ctx'), 'tensor')
- output_mean_new: float32 [768, 768], P('tensor', ('fsdp', 'ctx'))
- output_square_new: float32 [768, 768], P('tensor', ('fsdp', 'ctx'))
- up_mean_new: float32 [768, 3072], P(('fsdp', 'ctx'), 'tensor')
- up_square_new: float32 [768, 3072], P(('fsdp', 'ctx'), 'tensor')
- down_mean_new: float32 [3072, 768], P('tensor', ('fsdp', 'ctx'))
- down_square_new: float32 [3072, 768], P('tensor', ('fsdp', 'ctx'))
- vector_mean_new: float32 [12, 768], replicated
- vector_square_new: float32 [12, 768], replicated
Inputs may be any that keep to these rules, and one draw needn't show every extreme that they name: `attend_weight`: the three stacked projections of query, key and value; entries are of order 768 ** -0.5. `vectors`: rows 0 and 5 are the two norms' gains, between 0.4 and 1.6; the other rows are biases of order one.
All inputs are finite; a program needn't handle non-finite values.
Results may differ from a plain program's by a relative error of at most 0.007.
The roundings to bfloat16 on the way count: a program that leaves them out, or rounds other values in their place, can miss the bound.
Values may be sent and summed in bfloat16 or wider, within the bound.
No kernel may reach another device: no remote copies, remote signals or barrier semaphores. Data moves between devices by JAX's collectives and lax.ppermute only.
A program may use at most 128 MiB of HBM per device.

v0:
```python
import jax
import jax.numpy as jnp
from jax import lax
from jax.experimental import pallas as pl
from jax.experimental.pallas import tpu as pltpu
from jax.sharding import PartitionSpec as P


HD = 64
STEP = 3
CORES = 2

norm_eps = 1e-05
learn_rate = 0.04
beta_one = 0.9
beta_two = 0.999
adam_eps = 1e-08
decay_rate = 0.01
root_half = 0.7071067811865476
inv_root_tau = 0.3989422804014327

AXES = ("fsdp", "ctx", "tensor")
f32 = jnp.float32
bf16 = jnp.bfloat16


def layer_norm(inputs, gain_row, shift_row):
    row_mean = jnp.mean(inputs, -1, keepdims=True)
    centred = inputs - row_mean
    variance = jnp.mean(centred * centred, -1, keepdims=True)
    inv_scale = lax.rsqrt(variance + norm_eps)
    normed = centred * inv_scale
    return (normed * gain_row + shift_row, normed, inv_scale)


def norm_back(upstream, normed, inv_scale, gain_row):
    dnormed = upstream * gain_row
    mean_one = jnp.mean(dnormed, -1, keepdims=True)
    mean_two = jnp.mean(dnormed * normed, -1, keepdims=True)
    return inv_scale * (dnormed - mean_one - normed * mean_two)


def adamw(weight_now, gradient, mean_old, square_old, decay):
    mean_new = beta_one * mean_old + (1.0 - beta_one) * gradient
    square_new = beta_two * square_old + (1.0 - beta_two) * gradient * gradient
    mean_hat = mean_new / (1.0 - beta_one**STEP)
    square_hat = square_new / (1.0 - beta_two**STEP)
    weight_new = weight_now - learn_rate * (
        mean_hat / (jnp.sqrt(square_hat) + adam_eps) + decay * weight_now
    )
    return (weight_new, mean_new, square_new)


def dot(a, b, ca, cb):
    return lax.dot_general(a, b, (((ca,), (cb,)), ((), ())), preferred_element_type=f32)


def add_dot(total, a, b, ca, cb):
    part = dot(a, b, ca, cb)
    return part if total is None else total + part


class Layout:
    def __init__(self, outer, ctx, rows):
        self.outer, self.ctx, self.rows = outer, ctx, rows
        self.count = outer * ctx
        self.total = self.count * CORES * rows

    def offset(self, place, ctx_first, other, j):
        if ctx_first:
            jy, jf = j % self.ctx, j // self.ctx
        else:
            jf, jy = j % self.outer, j // self.outer
        block = ((place[0] ^ jf) * CORES + (place[1] ^ other)) * self.ctx + (place[2] ^ jy)
        return pl.multiple_of(block * self.rows, self.rows)

    def scratch(self, width):
        kind = bf16 if self.rows % 16 == 0 else f32
        return pltpu.VMEM((self.total, width), kind)

    def join(self, place, ctx_first, mine, theirs, plane, target):
        for other, ref in enumerate((mine, theirs)):
            for j in range(self.count):
                rows = pl.ds(self.offset(place, ctx_first, other, j), self.rows)
                target[rows, :] = ref[j, plane].astype(target.dtype)

    def cut(self, place, ctx_first, source, mine, theirs, plane):
        for other, ref in enumerate((mine, theirs)):
            for j in range(self.count):
                rows = pl.ds(self.offset(place, ctx_first, other, j), self.rows)
                ref[j, plane] = source[rows, :].astype(bf16)


def whole(*shape):
    return pl.BlockSpec(shape, lambda i, s: (0,) * len(shape))


def call(body, grid, in_specs, out_specs, out_shape, scratch, flops, trans, moved, mib):
    return pl.pallas_call(
        body,
        grid_spec=pltpu.PrefetchScalarGridSpec(
            num_scalar_prefetch=1,
            grid=grid,
            in_specs=in_specs,
            out_specs=out_specs,
            scratch_shapes=scratch,
        ),
        out_shape=out_shape,
        compiler_params=pltpu.CompilerParams(vmem_limit_bytes=mib * 1024 * 1024),
        cost_estimate=pl.CostEstimate(flops=flops, transcendentals=trans, bytes_accessed=moved),
    )


def project_body(
    layout, place, x0, x1, x2, x3, ma, ta, mb, tb, vec_ref, bias_ref, x_ref, h_ref, q_ref, kv_ref, w_ref, joined
):
    count = x0.shape[0]
    for j, ref in enumerate((x0, x1, x2, x3)):
        rows = slice(j * count, (j + 1) * count)
        x_ref[rows, :] = ref[...]
        norm_out, _, _ = layer_norm(ref[...].astype(f32), vec_ref[0:1, :], vec_ref[1:2, :])
        h_ref[rows, :] = norm_out.astype(bf16)
    for plane in range(4):
        first = plane < 2
        layout.join(place, first, ma if first else mb, ta if first else tb, plane % 2, joined)
        weight = joined[...].astype(bf16)
        w_ref[plane] = weight
        if plane == 3:
            break
        out = dot(h_ref[...], weight, 1, 0)
        if plane == 0:
            q_ref[...] = (out + bias_ref[0:1, :]).astype(bf16)
        elif plane == 1:
            kv_ref[0] = out.astype(bf16)
        else:
            kv_ref[1] = (out + bias_ref[1:2, :]).astype(bf16)


def project(layout, place, x_pieces, pieces, vectors, biases):
    step, width = x_pieces[0].shape
    rows = step * len(x_pieces)
    frames = whole(rows, width)
    return call(
        lambda *refs: project_body(layout, *refs),
        (1,),
        [whole(step, width)] * len(x_pieces)
        + [whole(*pieces[0].shape)] * 4
        + [whole(*vectors.shape), whole(*biases.shape)],
        [frames, frames, frames, whole(2, rows, width), whole(4, width, width)],
        [jax.ShapeDtypeStruct((rows, width), bf16)] * 3
        + [
            jax.ShapeDtypeStruct((2, rows, width), bf16),
            jax.ShapeDtypeStruct((4, width, width), bf16),
        ],
        [layout.scratch(width)],
        6 * rows * width * width,
        0,
        16 * width * width + 10 * rows * width,
        32,
    )(place, *x_pieces, *pieces, vectors, biases)


def attend_forward_body(place, q_ref, own_ref, far_ref, o_ref, lse_ref):
    lane = lax.broadcasted_iota(jnp.int32, (1, 2 * HD), 1)
    queries = q_ref[...]
    val_t = (own_ref[1].T, far_ref[1].T)
    parts = []
    for head in range(2):
        mask = ((lane // HD) == head).astype(f32) * HD ** (-0.5)
        q_head = queries * mask.astype(bf16)
        s_a = dot(own_ref[0], q_head, 1, 1)
        s_b = dot(far_ref[0], q_head, 1, 1)
        top = jnp.maximum(
            jnp.max(s_a, 0, keepdims=True), jnp.max(s_b, 0, keepdims=True)
        )
        e_a = jnp.exp(s_a - top)
        e_b = jnp.exp(s_b - top)
        total = jnp.sum(e_a, 0, keepdims=True) + jnp.sum(e_b, 0, keepdims=True)
        lse_ref[0, head : head + 1, :] = top + jnp.log(total)
        inv = 1.0 / total
        rows = slice(head * HD, (head + 1) * HD)
        parts.append(
            dot(val_t[0][rows], (e_a * inv).astype(bf16), 1, 0)
            + dot(val_t[1][rows], (e_b * inv).astype(bf16), 1, 0)
        )
    o_ref[...] = jnp.concatenate(parts, 0).T.astype(bf16)


def attend_forward(place, queries, own, far):
    rows, width = queries.shape
    pairs = width // (2 * HD)
    block = pl.BlockSpec((rows, 2 * HD), lambda i, s: (0, i))
    both = pl.BlockSpec((2, rows, 2 * HD), lambda i, s: (0, 0, i))
    return call(
        attend_forward_body,
        (pairs,),
        [block, both, both],
        [block, pl.BlockSpec((1, 2, rows), lambda i, s: (i, 0, 0))],
        [
            jax.ShapeDtypeStruct((rows, width), bf16),
            jax.ShapeDtypeStruct((pairs, 2, rows), f32),
        ],
        [],
        8 * rows * rows * width,
        2 * rows * rows * width // HD,
        12 * rows * width,
        24,
    )(place, queries, own, far)


def attend_backward_body(
    place,
    q_ref,
    own_ref,
    far_ref,
    o_ref,
    do_ref,
    lse_ref,
    dq_ref,
    dkeep_ref,
    dgive_ref,
    sums_ref,
):
    lane = lax.broadcasted_iota(jnp.int32, (1, 2 * HD), 1)
    queries = q_ref[...]
    dcontext = do_ref[...]
    weighed = (dcontext.astype(f32) * o_ref[...].astype(f32)).T
    key_t = (own_ref[0].T, far_ref[0].T)
    dkeys = [None, None]
    dvals = [None, None]
    dq_parts = []
    for head in range(2):
        mask = ((lane // HD) == head).astype(f32)
        q_head = queries * (mask * HD ** (-0.5)).astype(bf16)
        do_head = dcontext * mask.astype(bf16)
        rows = slice(head * HD, (head + 1) * HD)
        delta = jnp.sum(weighed[rows], 0, keepdims=True)
        lse = lse_ref[0, head : head + 1, :]
        dq_head = None
        for part, ref in enumerate((own_ref, far_ref)):
            probs = jnp.exp(dot(ref[0], q_head, 1, 1) - lse)
            dprobs = dot(ref[1], do_head, 1, 1)
            dscores = (probs * (dprobs - delta)).astype(bf16)
            dvals[part] = add_dot(dvals[part], probs.astype(bf16), do_head, 1, 0)
            dkeys[part] = add_dot(dkeys[part], dscores, q_head, 1, 0)
            dq_head = add_dot(dq_head, key_t[part][rows], dscores, 1, 0)
        dq_parts.append(dq_head)
    dquery = jnp.concatenate(dq_parts, 0).T * HD ** (-0.5)
    dq_ref[...] = dquery.astype(bf16)
    dkeep_ref[0] = dkeys[0]
    dkeep_ref[1] = dvals[0]
    dgive_ref[0] = dkeys[1].astype(bf16)
    dgive_ref[1] = dvals[1].astype(bf16)
    sums_ref[0:1, :] = jnp.sum(dquery, 0, keepdims=True)
    sums_ref[1:2, :] = jnp.sum(dvals[0], 0, keepdims=True) + jnp.sum(dvals[1], 0, keepdims=True)


def attend_backward(place, queries, own, far, context, dcontext, lse):
    rows, width = queries.shape
    pairs = width // (2 * HD)
    block = pl.BlockSpec((rows, 2 * HD), lambda i, s: (0, i))
    both = pl.BlockSpec((2, rows, 2 * HD), lambda i, s: (0, 0, i))
    return call(
        attend_backward_body,
        (pairs,),
        [block, both, both, block, block, pl.BlockSpec((1, 2, rows), lambda i, s: (i, 0, 0))],
        [block, both, both, pl.BlockSpec((2, 2 * HD), lambda i, s: (0, i))],
        [
            jax.ShapeDtypeStruct((rows, width), bf16),
            jax.ShapeDtypeStruct((2, rows, width), f32),
            jax.ShapeDtypeStruct((2, rows, width), bf16),
            jax.ShapeDtypeStruct((2, width), f32),
        ],
        [],
        20 * rows * rows * width,
        2 * rows * rows * width // HD,
        32 * rows * width,
        32,
    )(place, queries, own, far, context, dcontext, lse)


TILE = 512


def tiles(width, *lead):
    return pl.BlockSpec(lead + (TILE, width), lambda i, s: (0,) * len(lead) + (i, 0))


def gather_sums(sums_ref, *rows):
    @pl.when(pl.program_id(0) == 0)
    def _():
        sums_ref[...] = jnp.zeros_like(sums_ref)

    for j, values in enumerate(rows):
        sums_ref[j : j + 1, :] += jnp.sum(values, 0, keepdims=True)


def mix_body(place, x_ref, o_ref, w_ref, vec_ref, x1_ref, h_ref):
    residual = x_ref[...].astype(f32) + dot(o_ref[...], w_ref[0], 1, 1) + vec_ref[4:5, :]
    x1_ref[...] = residual
    norm_out, _, _ = layer_norm(residual, vec_ref[5:6, :], vec_ref[6:7, :])
    h_ref[...] = norm_out.astype(bf16)


def mix(place, x_low, context, weights, vectors):
    rows, width = x_low.shape
    return call(
        mix_body,
        (rows // TILE,),
        [
            tiles(width),
            tiles(width),
            pl.BlockSpec((1, width, width), lambda i, s: (3, 0, 0)),
            whole(*vectors.shape),
        ],
        [tiles(width), tiles(width)],
        [jax.ShapeDtypeStruct((rows, width), f32), jax.ShapeDtypeStruct((rows, width), bf16)],
        [],
        2 * rows * width * width,
        0,
        2 * width * width + 10 * rows * width,
        20,
    )(place, x_low, context, weights, vectors)


def unmix_body(place, dh_ref, x1_ref, e_ref, w_ref, vec_ref, dx_ref, low_ref, do_ref, sums_ref):
    cot = e_ref[...].astype(f32)
    dnorm = dh_ref[...]
    _, normed, inv_scale = layer_norm(x1_ref[...], vec_ref[5:6, :], vec_ref[6:7, :])
    dresidual = cot + norm_back(dnorm, normed, inv_scale, vec_ref[5:6, :])
    dx_ref[...] = dresidual
    low = dresidual.astype(bf16)
    low_ref[...] = low
    do_ref[...] = dot(low, w_ref[0], 1, 0).astype(bf16)
    gather_sums(sums_ref, dresidual, dnorm * normed, dnorm, cot)


def unmix(place, dnorm, residual, cot, weights, vectors):
    rows, width = residual.shape
    return call(
        unmix_body,
        (rows // TILE,),
        [
            tiles(width),
            tiles(width),
            tiles(width),
            pl.BlockSpec((1, width, width), lambda i, s: (3, 0, 0)),
            whole(*vectors.shape),
        ],
        [tiles(width), tiles(width), tiles(width), whole(4, width)],
        [
            jax.ShapeDtypeStruct((rows, width), f32),
            jax.ShapeDtypeStruct((rows, width), bf16),
            jax.ShapeDtypeStruct((rows, width), bf16),
            jax.ShapeDtypeStruct((4, width), f32),
        ],
        [],
        2 * rows * width * width,
        0,
        2 * width * width + 18 * rows * width,
        24,
    )(place, dnorm, residual, cot, weights, vectors)


def hidden_body(
    layout,
    place,
    h_ref,
    e0,
    e1,
    e2,
    e3,
    x_ref,
    ma,
    ta,
    mb,
    tb,
    c1_ref,
    c2_ref,
    e_ref,
    out_ref,
    dh_ref,
    ga,
    fa,
    gb,
    fb,
    dc1_ref,
    h_t,
    e_t,
    total,
    up_ref,
    down_ref,
    grad_ref,
):
    step = pl.program_id(0)

    @pl.when(step == 0)
    def _():
        count = e0.shape[0]
        for j, ref in enumerate((e0, e1, e2, e3)):
            rows = slice(j * count, (j + 1) * count)
            e_ref[rows, :] = ref[...]
            e_t[:, rows] = ref[...].T
        h_t[...] = h_ref[...].T
        total[...] = x_ref[...] + c2_ref[...]
        dh_ref[...] = jnp.zeros_like(dh_ref)

    layout.join(place, True, ma, ta, 0, up_ref)
    layout.join(place, False, mb, tb, 0, down_ref)
    up = up_ref[...].astype(bf16)
    down = down_ref[...].astype(bf16)
    pre_act = dot(h_ref[...], up, 1, 0) + c1_ref[0]
    half = 0.5 * (1.0 + lax.erf(pre_act * root_half))
    hidden = (pre_act * half).astype(bf16)
    slope = half + pre_act * jnp.exp(-0.5 * pre_act * pre_act) * inv_root_tau
    total[...] += dot(hidden, down, 1, 1)
    dpre = dot(e_ref[...], down, 1, 0) * slope
    dc1_ref[0] = jnp.sum(dpre, 0, keepdims=True)
    dpre_low = dpre.astype(bf16)
    grad_ref[...] = dot(e_t[...], hidden, 1, 0).astype(grad_ref.dtype)
    layout.cut(place, False, grad_ref, gb, fb, 0)
    grad_ref[...] = dot(h_t[...], dpre_low, 1, 0).astype(grad_ref.dtype)
    layout.cut(place, True, grad_ref, ga, fa, 0)
    dh_ref[...] += dot(dpre_low, up, 1, 1)

    @pl.when(step == pl.num_programs(0) - 1)
    def _():
        out_ref[...] = total[...].astype(bf16)


def hidden_both(layout, place, h_low, e_pieces, residual, pieces, c1_rows, c2_row):
    rows, width = h_low.shape
    count, blocks, block_rows, units = pieces[0].shape
    frames = whole(rows, width)
    piece = pl.BlockSpec((count, 1, block_rows, units), lambda i, s: (0, i, 0, 0))
    bias = pl.BlockSpec((1, 1, units), lambda i, s: (s[3] ^ i, 0, 0))
    return call(
        lambda *refs: hidden_body(layout, *refs),
        (blocks,),
        [frames]
        + [whole(*each.shape) for each in e_pieces]
        + [frames]
        + [piece] * 4
        + [bias, whole(1, width)],
        [frames, frames, frames] + [piece] * 4 + [bias],
        [
            jax.ShapeDtypeStruct((rows, width), bf16),
            jax.ShapeDtypeStruct((rows, width), bf16),
            jax.ShapeDtypeStruct((rows, width), f32),
        ]
        + [jax.ShapeDtypeStruct(pieces[0].shape, bf16)] * 4
        + [jax.ShapeDtypeStruct((blocks, 1, units), f32)],
        [
            pltpu.VMEM((width, rows), bf16),
            pltpu.VMEM((width, rows), bf16),
            pltpu.VMEM((rows, width), f32),
            layout.scratch(units),
            layout.scratch(units),
            layout.scratch(units),
        ],
        12 * rows * width * units * blocks,
        2 * rows * units * blocks,
        8 * width * units * blocks + 14 * rows * width,
        46,
    )(place, h_low, *e_pieces, residual, *pieces, c1_rows[:, None, :], c2_row[None])


def weigh_body(
    layout, place, h_ref, dq_ref, dkeep_ref, din_ref, dx_ref, o_ref, d_ref, ga, fa, gb, fb, grad_ref
):
    h_t = h_ref[...].T
    for plane in range(4):
        if plane == 0:
            d_ref[0] = dq_ref[...]
        elif plane < 3:
            part = dkeep_ref[plane - 1] + din_ref[plane - 1].astype(f32)
            d_ref[plane] = part.astype(bf16)
        if plane < 3:
            grad = dot(h_t, d_ref[plane], 1, 0)
        else:
            grad = dot(dx_ref[...].T, o_ref[...], 1, 0)
        grad_ref[...] = grad.astype(grad_ref.dtype)
        first = plane < 2
        layout.cut(place, first, grad_ref, ga if first else gb, fa if first else fb, plane % 2)


def weigh(layout, place, h_low, dquery, dkeep, din, dx_low, context):
    rows, width = h_low.shape
    frames = whole(rows, width)
    shape = (layout.count, 2, layout.rows, width)
    return call(
        lambda *refs: weigh_body(layout, *refs),
        (1,),
        [frames, frames, whole(2, rows, width), whole(2, rows, width), frames, frames],
        [whole(3, rows, width)] + [whole(*shape)] * 4,
        [jax.ShapeDtypeStruct((3, rows, width), bf16)] + [jax.ShapeDtypeStruct(shape, bf16)] * 4,
        [layout.scratch(width)],
        8 * rows * width * width,
        0,
        8 * width * width + 28 * rows * width,
        36,
    )(place, h_low, dquery, dkeep, din, dx_low, context)


def finish_body(place, d_ref, w_ref, x_ref, dx_ref, vec_ref, out_ref, sums_ref):
    dnorm = None
    for plane in range(3):
        dnorm = add_dot(dnorm, d_ref[plane], w_ref[plane], 1, 1)
    _, normed, inv_scale = layer_norm(x_ref[...].astype(f32), vec_ref[0:1, :], vec_ref[1:2, :])
    out = dx_ref[...] + norm_back(dnorm, normed, inv_scale, vec_ref[0:1, :])
    out_ref[...] = out.astype(bf16)
    gather_sums(sums_ref, dnorm * normed, dnorm)


def finish(place, dproj, weights, x_low, dresidual, vectors):
    rows, width = x_low.shape
    return call(
        finish_body,
        (rows // TILE,),
        [
            tiles(width, 3),
            whole(3, width, width),
            tiles(width),
            tiles(width),
            whole(*vectors.shape),
        ],
        [tiles(width), whole(2, width)],
        [jax.ShapeDtypeStruct((rows, width), bf16), jax.ShapeDtypeStruct((2, width), f32)],
        [],
        6 * rows * width * width,
        0,
        6 * width * width + 14 * rows * width,
        28,
    )(place, dproj, weights, x_low, dresidual, vectors)


def update(refs, gradient):
    out = (gradient,) + adamw(refs[0][...], gradient, refs[1][...], refs[2][...], decay_rate)
    for ref, values in zip(refs[3:], out):
        ref[...] = values


def update_ff_body(place, *refs):
    terms, refs = refs[:-14], refs[-14:]
    total = sum(term[...].astype(f32) for term in terms)
    update(refs[0:3] + refs[6:10], total[0, 0])
    update(refs[3:6] + refs[10:14], total[1, 0])


def update_proj_body(place, *refs):
    terms, refs = refs[:-14], refs[-14:]
    total = sum(term[...].astype(f32) for term in terms)
    update(refs[0:3] + refs[6:10], total[:3])
    update(refs[3:6] + refs[10:14], total[3].T)


def update_both(place, body, terms, first, second):
    shapes = [first[0].shape] * 4 + [second[0].shape] * 4
    inputs = list(terms) + list(first) + list(second)
    out = call(
        body,
        (1,),
        [whole(*each.shape) for each in inputs],
        [whole(*shape) for shape in shapes],
        [jax.ShapeDtypeStruct(shape, f32) for shape in shapes],
        [],
        0,
        first[0].size + second[0].size,
        32 * (first[0].size + second[0].size),
        20,
    )(place, *inputs)
    return out[:4], out[4:]


def bits(count):
    step = 1
    while step < count:
        yield step
        step *= 2


class Grid:
    def __init__(self):
        self.fsdp = lax.axis_size("fsdp")
        self.outer = self.fsdp // CORES
        self.ctx = lax.axis_size("ctx")
        self.tensor = lax.axis_size("tensor")
        here = lax.axis_index(AXES)
        self.place = lax.rem(
            here // jnp.array([CORES * self.ctx * self.tensor, self.ctx * self.tensor, self.tensor, 1]),
            jnp.array([self.outer, CORES, self.ctx, self.tensor]),
        ).astype(jnp.int32)
        self.z = lax.axis_index("tensor")

    def index(self, fo, core, y, z):
        return ((fo * CORES + core) * self.ctx + y) * self.tensor + z

    def move(self, data, target):
        pairs = []
        for fo in range(self.outer):
            for core in range(CORES):
                for y in range(self.ctx):
                    for z in range(self.tensor):
                        pairs.append((self.index(fo, core, y, z), self.index(*target(fo, core, y, z))))
        return lax.ppermute(data, AXES, pairs)

    def swap(self, data, axis, bit=1):
        dim = ("x", "core", "y", "z").index(axis)
        return self.move(data, lambda *at: tuple(v ^ bit if i == dim else v for i, v in enumerate(at)))

    def turn(self, rows):
        for bit in bits(self.tensor):
            order = [j ^ bit for j in range(self.tensor)]
            other = jnp.stack([rows[j] for j in order])
            rows = jnp.where((self.z & bit) != 0, other, rows)
        return rows


def over_tensor(grid, shard):
    data = shard[None]
    for bit in bits(grid.tensor):
        data = jnp.concatenate([data, grid.swap(data, "z", bit)], 0)
    return data


def axis_bits(grid, ctx_first):
    outer = [("x", bit) for bit in bits(grid.outer)]
    inner = [("y", bit) for bit in bits(grid.ctx)]
    return inner + outer if ctx_first else outer + inner


def spread(grid, planes, ctx_first):
    data = planes[None]
    for axis, bit in axis_bits(grid, ctx_first):
        data = jnp.concatenate([data, grid.swap(data, axis, bit)], 0)
    return data, grid.swap(data, "core")


def collect(grid, keep, give, ctx_first):
    terms = [keep, grid.swap(give, "core")]
    for axis, bit in reversed(axis_bits(grid, ctx_first)):
        half = terms[0].shape[0] // 2
        out = sum(term[half:].astype(f32) for term in terms).astype(bf16)
        terms = [term[:half] for term in terms] + [grid.swap(out, axis, bit)]
    return [term[0] for term in terms]


def total_of(terms):
    return sum(term.astype(f32) for term in terms)


def to_owner(grid, terms, split):
    for bit in reversed(list(bits(grid.tensor))):
        halves = [split(term, bit) for term in terms]
        out = total_of([half[1] for half in halves]).astype(bf16)
        terms = [half[0] for half in halves] + [grid.swap(out, "z", bit)]
    return terms


def sum_everywhere(grid, rows):
    rows = rows + grid.swap(rows, "core")
    for axis, count in (("x", grid.outer), ("y", grid.ctx), ("z", grid.tensor)):
        for bit in bits(count):
            rows = rows + grid.swap(rows, axis, bit)
    return rows


def clips_in(grid, frames):
    pieces = []
    for j in range(grid.tensor):
        out = lax.dynamic_index_in_dim(frames, grid.z ^ j, 0, False)
        pieces.append(grid.move(out, lambda f, c, y, z: (f, y, c, z ^ j)))
    return pieces


def clips_out_body(place, *refs):
    out_ref = refs[-1]
    for j, ref in enumerate(refs[:-1]):
        out_ref[pl.ds(place[3] ^ j, 1)] = ref[...].astype(out_ref.dtype)[None]


def clips_out(grid, rows, kind):
    step = rows.shape[0] // grid.tensor
    pieces = []
    for j in range(grid.tensor):
        out = rows[j * step : (j + 1) * step]
        pieces.append(grid.move(out, lambda f, c, y, z: (f, y, c, z ^ j)))
    shape = (step, rows.shape[1])
    return call(
        clips_out_body,
        (1,),
        [whole(*shape)] * grid.tensor,
        whole(grid.tensor, *shape),
        jax.ShapeDtypeStruct((grid.tensor,) + shape, kind),
        [],
        0,
        0,
        8 * rows.size,
        10,
    )(grid.place, *pieces)


def step_of(
    frames_in,
    out_cotangent,
    attend_weight,
    output_weight,
    up_weight,
    down_weight,
    vectors,
    attend_mean,
    attend_square,
    output_mean,
    output_square,
    up_mean,
    up_square,
    down_mean,
    down_square,
    vector_mean,
    vector_square,
):
    grid = Grid()
    place = grid.place
    width = frames_in.shape[2]
    part = attend_weight.shape[2]
    layout = Layout(grid.outer, grid.ctx, up_weight.shape[0])

    shard = jnp.concatenate([attend_weight.astype(bf16), output_weight.astype(bf16).T[None]], 0)
    proj = over_tensor(grid, shard)
    proj = jnp.concatenate([proj[j] for j in range(grid.tensor)], 2)
    x_pieces = clips_in(grid, frames_in)
    proj_pieces = spread(grid, proj[:2], True) + spread(grid, proj[2:], False)
    shard = jnp.stack([up_weight.astype(bf16), down_weight.astype(bf16).T])
    ff = over_tensor(grid, shard)
    ff_pieces = spread(grid, ff[:, 0], True) + spread(grid, ff[:, 1], False)
    e_pieces = clips_in(grid, out_cotangent)

    def turned(row):
        return grid.turn(row.reshape(grid.tensor, part)).reshape(1, width)

    biases = jnp.concatenate([turned(vectors[2]), turned(vectors[3])], 0)

    x_low, in_norm1, queries, own, weights = project(
        layout, place, x_pieces, proj_pieces, vectors, biases
    )
    far = grid.swap(own, "core")
    context, log_total = attend_forward(place, queries, own, far)
    residual, in_norm2 = mix(place, x_low, context, weights, vectors)
    cot_low, result, dnorm2, ga, fa, gb, fb, grad_c1 = hidden_both(
        layout, place, in_norm2, e_pieces, residual, ff_pieces, vectors[8:12], vectors[7]
    )
    frames_out = clips_out(grid, result, bf16)
    ff_a = collect(grid, ga, fa, True)
    ff_b = collect(grid, gb, fb, False)

    dresidual, dres_low, dcontext, mid_sums = unmix(
        place, dnorm2, residual, cot_low, weights, vectors
    )
    dquery, dkeep, dgive, sums = attend_backward(
        place, queries, own, far, context, dcontext, log_total
    )
    din = grid.swap(dgive, "core")
    dproj, ga, fa, gb, fb = weigh(layout, place, in_norm1, dquery, dkeep, din, dres_low, context)
    proj_a = collect(grid, ga, fa, True)
    proj_b = collect(grid, gb, fb, False)
    dinputs, end_sums = finish(place, dproj, weights, x_low, dresidual, vectors)
    frames_grad = clips_out(grid, dinputs, f32)

    vector_part = jnp.concatenate(
        [end_sums, jnp.stack([turned(sums[0])[0], turned(sums[1])[0]]), mid_sums, grad_c1[:, 0, :]],
        0,
    )
    vector_grad = sum_everywhere(grid, vector_part)

    def by_block(term, bit):
        return term[:, :bit], term[:, bit:]

    def by_column(term, bit):
        return term[..., : bit * part], term[..., bit * part :]

    terms = to_owner(grid, [jnp.stack(pair) for pair in zip(ff_a, ff_b)], by_block)
    ups, downs = update_both(
        place,
        update_ff_body,
        terms,
        (up_weight, up_mean, up_square),
        (down_weight.T, down_mean.T, down_square.T),
    )
    up_grad, up_new, up_mean_new, up_square_new = ups
    down_grad, down_new, down_mean_new, down_square_new = [each.T for each in downs]
    terms = to_owner(grid, [jnp.concatenate(pair, 0) for pair in zip(proj_a, proj_b)], by_column)
    attends, outputs = update_both(
        place,
        update_proj_body,
        terms,
        (attend_weight, attend_mean, attend_square),
        (output_weight, output_mean, output_square),
    )
    attend_grad, attend_new, attend_mean_new, attend_square_new = attends
    output_grad, output_new, output_mean_new, output_square_new = outputs
    vector_new, vector_mean_new, vector_square_new = adamw(
        vectors, vector_grad, vector_mean, vector_square, 0.0
    )
    return (
        frames_out,
        frames_grad,
        attend_grad,
        output_grad,
        up_grad,
        down_grad,
        vector_grad,
        attend_new,
        output_new,
        up_new,
        down_new,
        vector_new,
        attend_mean_new,
        attend_square_new,
        output_mean_new,
        output_square_new,
        up_mean_new,
        up_square_new,
        down_mean_new,
        down_square_new,
        vector_mean_new,
        vector_square_new,
    )


def solution(mesh):
    frames = P("fsdp", ("ctx", "tensor"), None)
    attend = P(None, ("fsdp", "ctx"), "tensor")
    tall = P("tensor", ("fsdp", "ctx"))
    flat = P(("fsdp", "ctx"), "tensor")
    weights = (attend, tall, flat, tall)
    return jax.shard_map(
        step_of,
        mesh=mesh,
        in_specs=(frames, frames)
        + weights
        + (P(), attend, attend, tall, tall, flat, flat, tall, tall, P(), P()),
        out_specs=(frames, frames)
        + weights
        + (P(),)
        + weights
        + (P(), attend, attend, tall, tall, flat, flat, tall, tall, P(), P()),
        check_vma=False,
    )
```

profile of v0, /device:TPU:0, one launch (start us, length us, event | category | flops | bytes accessed | tf_op | source)
XLA Modules:
  0.0 424.2 jit_solution(9260012039585737920)
XLA Ops:
  2.8 3.1 collective-permute-start.4
  6.1 5.6 %collective-permute-done.4 = bf16[1,4,96,192]{3,2,1,0:T(8,128)(2,1)S(1)} collective-permute-done((bf16[1,4,96,192]{3,2,1,0:T(8,128)(2,1)S(1)}, bf16[1,4,96,192]{3,2,1,0:T(8,128)(2,1)S(1)}, u32[]{:S(2)}, u32[]{:S(2)}) %collective-permute-start.4) | collective-permute-done | bytes 147488 | tf_op jit(solution)/shard_map/ppermute | solution.py:605
  11.7 3.1 collective-permute-start.5
  17.0 5.7 %collective-permute-done.17 = bf16[1,2,96,768]{3,2,0,1:T(8,128)(2,1)S(1)} collective-permute-done((bf16[1,2,96,768]{3,2,0,1:T(8,128)(2,1)S(1)}, bf16[1,2,96,768]{3,2,0,1:T(8,128)(2,1)S(1)}, u32[]{:S(2)}, u32[]{:S(2)}) %collective-permute-start.17) | collective-permute-done | bytes 294944 | tf_op jit(solution)/shard_map/ppermute | solution.py:605
  22.9 27.1 %collective-permute-done.5 = bf16[2,4,96,192]{3,2,1,0:T(8,128)(2,1)S(1)} collective-permute-done((bf16[2,4,96,192]{3,2,1,0:T(8,128)(2,1)S(1)}, bf16[2,4,96,192]{3,2,1,0:T(8,128)(2,1)S(1)}, u32[]{:S(2)}, u32[]{:S(2)}) %collective-permute-start.5) | collective-permute-done | bytes 294944 | tf_op jit(solution)/shard_map/ppermute | solution.py:605
  52.5 11.8 %collective-permute-done.18 = bf16[2,2,96,768]{3,2,0,1:T(8,128)(2,1)S(1)} collective-permute-done((bf16[2,2,96,768]{3,2,0,1:T(8,128)(2,1)S(1)}, bf16[2,2,96,768]{3,2,0,1:T(8,128)(2,1)S(1)}, u32[]{:S(2)}, u32[]{:S(2)}) %collective-permute-start.18) | collective-permute-done | bytes 589856 | tf_op jit(solution)/shard_map/ppermute | solution.py:605
  68.3 1.9 pad_maximum_fusion.9
  71.6 4.4 %collective-permute-done.6 = bf16[1,2,96,768]{3,2,1,0:T(8,128)(2,1)S(1)} collective-permute-done((bf16[1,2,96,768]{3,2,1,0:T(8,128)(2,1)S(1)}, bf16[1,2,96,768]{3,2,1,0:T(8,128)(2,1)S(1)}, u32[]{:S(2)}, u32[]{:S(2)}) %collective-permute-start.6) | collective-permute-done | bytes 294944 | tf_op jit(solution)/shard_map/ppermute | solution.py:605
  77.6 3.2 collective-permute-done.22
  83.4 5.2 %collective-permute-done.19 = bf16[1,4,96,768]{3,2,1,0:T(8,128)(2,1)S(1)} collective-permute-done((bf16[1,4,96,768]{3,2,1,0:T(8,128)(2,1)S(1)}, bf16[1,4,96,768]{3,2,1,0:T(8,128)(2,1)S(1)}, u32[]{:S(2)}, u32[]{:S(2)}) %collective-permute-start.19) | collective-permute-done | bytes 589856 | tf_op jit(solution)/shard_map/ppermute | solution.py:605
  90.8 2.7 collective-permute-done.7
  94.8 6.6 %collective-permute-done.10 = bf16[2,2,96,768]{3,2,1,0:T(8,128)(2,1)} collective-permute-done((bf16[2,2,96,768]{3,2,1,0:T(8,128)(2,1)}, bf16[2,2,96,768]{3,2,1,0:T(8,128)(2,1)}, u32[]{:S(2)}, u32[]{:S(2)}) %collective-permute-start.10) | collective-permute-done | bytes 589856 | tf_op jit(solution)/shard_map/ppermute | solution.py:605
  102.9 20.0 %collective-permute-done.23 = bf16[2,4,96,768]{3,2,1,0:T(8,128)(2,1)} collective-permute-done((bf16[2,4,96,768]{3,2,1,0:T(8,128)(2,1)}, bf16[2,4,96,768]{3,2,1,0:T(8,128)(2,1)}, u32[]{:S(2)}, u32[]{:S(2)}) %collective-permute-start.23) | collective-permute-done | bytes 1179680 | tf_op jit(solution)/shard_map/ppermute | solution.py:605
  123.7 3.3 pad_maximum_fusion.1.refs_9_
  128.7 2.9 pad_maximum_fusion.refs_7_
  134.5 3.4 collective-permute-start.2
  138.1 9.8 %collective-permute-done.2.refs_3_ = bf16[128,768]{1,0:T(8,128)(2,1)S(1)} collective-permute-done((bf16[128,768]{1,0:T(8,128)(2,1)}, bf16[128,768]{1,0:T(8,128)(2,1)S(1)}, u32[]{:S(2)}, u32[]{:S(2)}) %collective-permute-start.2) | collective-permute-done | bytes 196640 | tf_op jit(solution)/shard_map/ppermute | solution.py:605
  149.7 5.2 %shard_map.354 = (bf16[512,768]{1,0:T(8,128)(2,1)S(1)}, bf16[512,768]{1,0:T(8,128)(2,1)S(1)}, bf16[512,768]{1,0:T(8,128)(2,1)S(1)}, bf16[2,512,768]{2,1,0:T(8,128)(2,1)S(1)}, bf16[4,768,768]{2,1,0:T(8,128)(2,1)S(1)}) custom-call(s32[4]{0:T(128)S(1)} %fusion.12.refs_0_.place, bf16[128,768]{1,0:T(8,128)(2,1)S(1)} %copy-done.34, ...), custom_call_target="tpu_custom_call" | custom-call | flops 1811939328 | bytes 13369344 | tf_op jit(solution)/shard_map/pallas_call | solution.py:143
  155.5 2.5 collective-permute-start.16
  158.1 7.2 %collective-permute-done.16.refs_5_ = bf16[128,768]{1,0:T(8,128)(2,1)S(1)} collective-permute-done((bf16[128,768]{1,0:T(8,128)(2,1)S(1)}, bf16[128,768]{1,0:T(8,128)(2,1)S(1)}, u32[]{:S(2)}, u32[]{:S(2)}) %collective-permute-start.16) | collective-permute-done | bytes 196640 | tf_op jit(solution)/shard_map/ppermute | solution.py:605
  167.3 13.8 %shard_map.355 = (bf16[512,768]{1,0:T(8,128)(2,1)S(1)}, f32[6,2,512]{2,1,0:T(2,128)S(1)}) custom-call(s32[4]{0:T(128)S(1)} %fusion.12.refs_0_.place, bf16[512,768]{1,0:T(8,128)(2,1)S(1)} %get-tuple-element.71.q_ref, bf16[2,512,768]{2,1,0:T(8,128)(2,1)S(1)} %get-tuple-element.72.own_ref, bf16[2,512,768]{2,1,0:T(8,128)(2,1)S(1)} %collective-permute-done.12.far_ref), custom_call_target="tpu_custom_call" | custom-call | flops 1610612736 | bytes 4718592 | tf_op jit(solution)/shard_map/pallas_call | solution.py:194
  181.1 1.8 shard_map.356
  183.0 22.3 %shard_map.357 = (bf16[512,768]{1,0:T(8,128)(2,1)S(1)}, bf16[512,768]{1,0:T(8,128)(2,1)S(1)}, f32[512,768]{1,0:T(8,128)S(1)}, bf16[4,4,96,768]{3,2,1,0:T(8,128)(...) custom-call(s32[4]{0:T(128)S(1)} %fusion.12.refs_0_.place, ...), custom_call_target="tpu_custom_call" | custom-call | flops 14495514624 | bytes 24379392 | tf_op jit(solution)/shard_map/pallas_call | solution.py:437
  206.1 2.0 collective-permute-start.28
  208.9 2.5 shard_map.359
  211.4 20.5 %shard_map.360 = (bf16[512,768]{1,0:T(8,128)(2,1)S(1)}, f32[2,512,768]{2,1,0:T(8,128)S(1)}, bf16[2,512,768]{2,1,0:T(8,128)(2,1)}, f32[2,768]{1,0:T(2,128)S(1)}) custom-call(s32[4]{0:T(128)S(1)} %fusion.12.refs_0_.place, bf16[512,768]{1,0:T(8,128)(2,1)S(1)} %get-tuple-element.71.q_ref, bf16[2,512,768]{2,1,0:T(8,128)(2,1)S(1)} %get-tuple-element.72.own_ref, ...), custom_call_target="tpu_custom_call" | custom-call | flops 4026531840 | bytes 12582912 | tf_op jit(solution)/shard_map/pallas_call | solution.py:263
  234.5 4.4 %collective-permute-start.29 = (bf16[2,512,768]{2,1,0:T(8,128)(2,1)}, bf16[2,512,768]{2,1,0:T(8,128)(2,1)}, u32[]{:S(2)}, u32[]{:S(2)}) collective-permute-start(bf16[2,512,768]{2,1,0:T(8,128)(2,1)} %get-tuple-element.85), channel_id=1, source_target_pairs={{0,8},{1,9},{2,10},{3,11},{4,12},{5,13},{6,14},{7,15},{8,0},{9,1},... | collective-permute-start | bytes 4718600 | tf_op jit(solution)/shard_map/ppermute | solution.py:605
  244.9 1.9 copy-done.36
  249.1 4.9 %shard_map.361 = (bf16[3,512,768]{2,1,0:T(8,128)(2,1)S(1)}, bf16[4,2,96,768]{3,2,1,0:T(8,128)(2,1)S(1)}, bf16[4,2,96,768]{3,2,1,0:T(8,128)(2,1)S(1)}, bf16[4,2,9...) custom-call(s32[4]{0:T(128)S(1)} %fusion.12.refs_0_.place, bf16[512,768]{1,0:T(8,128)(2,1)S(1)} %copy-done.38, ...), custom_call_target="tpu_custom_call" | custom-call | flops 2415919104 | bytes 15728640 | tf_op jit(solution)/shard_map/pallas_call | solution.py:491
  255.1 3.2 shard_map.362
  263.5 3.2 collective-permute-done.51
  270.5 2.1 collective-permute-start.52
  272.7 2.5 shard_map.358
  275.4 2.7 collective-permute-start.33
  281.1 17.9 %collective-permute-done.54 = f32[12,768]{1,0:T(8,128)S(1)} collective-permute-done((f32[12,768]{1,0:T(8,128)S(1)}, f32[12,768]{1,0:T(8,128)S(1)}, u32[]{:S(2)}, u32[]{:S(2)}) %collective-permute-start.54) | collective-permute-done | bytes 36896 | tf_op jit(solution)/shard_map/ppermute | solution.py:605
  300.3 6.3 %collective-permute-done.31.refs_1_ = bf16[128,768]{1,0:T(8,128)(2,1)S(1)} collective-permute-done((bf16[128,768]{1,0:T(8,128)(2,1)S(1)}, bf16[128,768]{1,0:T(8,128)(2,1)S(1)}, u32[]{:S(2)}, u32[]{:S(2)}) %collective-permute-start.31) | collective-permute-done | bytes 196640 | tf_op jit(solution)/shard_map/ppermute | solution.py:605
  307.4 1.8 shard_map.363
  309.2 1.7 add_convert_fusion.1
  313.2 1.8 collective-permute-start.45
  319.5 20.4 %collective-permute-done.44 = bf16[2,4,96,768]{3,2,1,0:T(8,128)(2,1)S(1)} collective-permute-done((bf16[2,4,96,768]{3,2,1,0:T(8,128)(2,1)S(1)}, bf16[2,4,96,768]{3,2,1,0:T(8,128)(2,1)S(1)}, u32[]{:S(2)}, u32[]{:S(2)}) %collective-permute-start.44) | collective-permute-done | bytes 1179680 | tf_op jit(solution)/shard_map/ppermute | solution.py:605
  344.8 7.6 %collective-permute-done.36 = bf16[2,2,96,768]{3,2,1,0:T(8,128)(2,1)S(1)} collective-permute-done((bf16[2,2,96,768]{3,2,1,0:T(8,128)(2,1)S(1)}, bf16[2,2,96,768]{3,2,1,0:T(8,128)(2,1)S(1)}, u32[]{:S(2)}, u32[]{:S(2)}) %collective-permute-start.36) | collective-permute-done | bytes 589856 | tf_op jit(solution)/shard_map/ppermute | solution.py:605
  356.4 10.9 %collective-permute-done.46 = bf16[1,4,96,768]{3,2,1,0:T(8,128)(2,1)S(1)} collective-permute-done((bf16[1,4,96,768]{3,2,1,0:T(8,128)(2,1)S(1)}, bf16[1,4,96,768]{3,2,1,0:T(8,128)(2,1)S(1)}, u32[]{:S(2)}, u32[]{:S(2)}) %collective-permute-start.46) | collective-permute-done | bytes 589856 | tf_op jit(solution)/shard_map/ppermute | solution.py:605
  368.1 4.8 %collective-permute-done.38 = bf16[1,2,96,768]{3,2,1,0:T(8,128)(2,1)S(1)} collective-permute-done((bf16[1,2,96,768]{3,2,1,0:T(8,128)(2,1)S(1)}, bf16[1,2,96,768]{3,2,1,0:T(8,128)(2,1)S(1)}, u32[]{:S(2)}, u32[]{:S(2)}) %collective-permute-start.38) | collective-permute-done | bytes 294944 | tf_op jit(solution)/shard_map/ppermute | solution.py:605
  374.0 28.8 %collective-permute-done.48 = bf16[2,2,96,768]{3,2,1,0:T(8,128)(2,1)S(1)} collective-permute-done((bf16[2,2,96,768]{3,2,1,0:T(8,128)(2,1)S(1)}, bf16[2,2,96,768]{3,2,1,0:T(8,128)(2,1)S(1)}, u32[]{:S(2)}, u32[]{:S(2)}) %collective-permute-start.48) | collective-permute-done | bytes 589856 | tf_op jit(solution)/shard_map/ppermute | solution.py:605
  403.0 4.9 %collective-permute-done.40 = bf16[4,96,384]{2,1,0:T(8,128)(2,1)S(1)} collective-permute-done((bf16[4,96,384]{2,1,0:T(8,128)(2,1)S(1)}, bf16[4,96,384]{2,1,0:T(8,128)(2,1)S(1)}, u32[]{:S(2)}, u32[]{:S(2)}) %collective-permute-start.40) | collective-permute-done | bytes 294944 | tf_op jit(solution)/shard_map/ppermute | solution.py:605
  408.6 9.8 %collective-permute-done.41.refs_5_ = bf16[4,96,192]{2,1,0:T(8,128)(2,1)S(1)} collective-permute-done((bf16[4,96,192]{2,1,0:T(8,128)(2,1)S(1)}, bf16[4,96,192]{2,1,0:T(8,128)(2,1)S(1)}, u32[]{:S(2)}, u32[]{:S(2)}) %collective-permute-start.41) | collective-permute-done | bytes 147488 | tf_op jit(solution)/shard_map/ppermute | solution.py:605
  418.4 2.3 shard_map.364
  422.0 2.3 shard_map.365
  (297 shorter events, 78.8 us)
Async XLA Ops:
  2.8 8.9 %collective-permute-start.4 = (bf16[1,4,96,192]{3,2,1,0:T(8,128)(2,1)S(1)}, bf16[1,4,96,192]{3,2,1,0:T(8,128)(2,1)S(1)}, u32[]{:S(2)}, u32[]{:S(2)}) collective-permute-start(bf16[1,4,96,192]{3,2,1,0:T(8,128)(2,1)S(1)} %maximum_bitcast_fusion.1), channel_id=1, source_target_pairs={{0,1},{1,0},{2,3},{3,2},{4,5},{5,4},{6,7},{7,6},{8,9},{9,8},{10,11... | collective-permute-start | bytes 442376 | tf_op jit(solution)/shard_map/ppermute | solution.py:605
  6.0 16.8 %collective-permute-start.17 = (bf16[1,2,96,768]{3,2,0,1:T(8,128)(2,1)S(1)}, bf16[1,2,96,768]{3,2,0,1:T(8,128)(2,1)S(1)}, u32[]{:S(2)}, u32[]{:S(2)}) collective-permute-start(bf16[1,2,96,768]{3,2,0,1:T(8,128)(2,1)S(1)} %maximum_bitcast_fusion), channel_id=1, source_target_pairs={{0,1},{1,0},{2,3},{3,2},{4,5},{5,4},{6,7},{7,6},{8,9},{9,8},{10,11... | collective-permute-start | bytes 884744 | tf_op jit(solution)/shard_map/ppermute | solution.py:605
  11.7 38.3 %collective-permute-start.5 = (bf16[2,4,96,192]{3,2,1,0:T(8,128)(2,1)S(1)}, bf16[2,4,96,192]{3,2,1,0:T(8,128)(2,1)S(1)}, u32[]{:S(2)}, u32[]{:S(2)}) collective-permute-start(bf16[2,4,96,192]{3,2,1,0:T(8,128)(2,1)S(1)} %pad_maximum_fusion.11), channel_id=1, source_target_pairs={{0,2},{1,3},{2,0},{3,1},{4,6},{5,7},{6,4},{7,5},{8,10},{9,11},{10,... | collective-permute-start | bytes 884744 | tf_op jit(solution)/shard_map/ppermute | solution.py:605
  15.7 115.9 %collective-permute-start.3 = (bf16[128,768]{1,0:T(8,128)(2,1)}, bf16[128,768]{1,0:T(8,128)(2,1)S(1)}, u32[]{:S(2)}, u32[]{:S(2)}) collective-permute-start(bf16[128,768]{1,0:T(8,128)(2,1)} %get-tuple-element.140), channel_id=1, source_target_pairs={{0,3},{1,2},{2,1},{3,0},{4,11},{5,10},{6,9},{7,8},{8,7},{9,6},{10,... | collective-permute-start | bytes 589832 | tf_op jit(solution)/shard_map/ppermute | solution.py:605
  22.8 41.4 %collective-permute-start.18 = (bf16[2,2,96,768]{3,2,0,1:T(8,128)(2,1)S(1)}, bf16[2,2,96,768]{3,2,0,1:T(8,128)(2,1)S(1)}, u32[]{:S(2)}, u32[]{:S(2)}) collective-permute-start(bf16[2,2,96,768]{3,2,0,1:T(8,128)(2,1)S(1)} %pad_maximum_fusion.10), channel_id=1, source_target_pairs={{0,2},{1,3},{2,0},{3,1},{4,6},{5,7},{6,4},{7,5},{8,10},{9,11},{10,... | collective-permute-start | bytes 1769480 | tf_op jit(solution)/shard_map/ppermute | solution.py:605
  51.1 17.2 %collective-permute-start.9 = (bf16[1,2,96,768]{3,2,1,0:T(8,128)(2,1)S(1)}, bf16[1,2,96,768]{3,2,1,0:T(8,128)(2,1)}, u32[]{:S(2)}, u32[]{:S(2)}) collective-permute-start(bf16[1,2,96,768]{3,2,1,0:T(8,128)(2,1)S(1)} %get-tuple-element.144), channel_id=1, source_target_pairs={{0,16},{1,17},{2,18},{3,19},{4,20},{5,21},{6,22},{7,23},{8,24},{9,... | collective-permute-start | bytes 884744 | tf_op jit(solution)/shard_map/ppermute | solution.py:605
  64.5 16.3 %collective-permute-start.22 = (bf16[1,4,96,768]{3,2,1,0:T(8,128)(2,1)S(1)}, bf16[1,4,96,768]{3,2,1,0:T(8,128)(2,1)S(1)}, u32[]{:S(2)}, u32[]{:S(2)}) collective-permute-start(bf16[1,4,96,768]{3,2,1,0:T(8,128)(2,1)S(1)} %get-tuple-element.126), channel_id=1, source_target_pairs={{0,16},{1,17},{2,18},{3,19},{4,20},{5,21},{6,22},{7,23},{8,24},{9,... | collective-permute-start | bytes 1769480 | tf_op jit(solution)/shard_map/ppermute | solution.py:605
  66.2 9.9 %collective-permute-start.6 = (bf16[1,2,96,768]{3,2,1,0:T(8,128)(2,1)S(1)}, bf16[1,2,96,768]{3,2,1,0:T(8,128)(2,1)S(1)}, u32[]{:S(2)}, u32[]{:S(2)}) collective-permute-start(bf16[1,2,96,768]{3,2,1,0:T(8,128)(2,1)S(1)} %copy-done.44), channel_id=1, source_target_pairs={{0,4},{1,5},{2,6},{3,7},{4,0},{5,1},{6,2},{7,3},{8,12},{9,13},{10,... | collective-permute-start | bytes 884744 | tf_op jit(solution)/shard_map/ppermute | solution.py:605
  67.7 21.0 %collective-permute-start.19 = (bf16[1,4,96,768]{3,2,1,0:T(8,128)(2,1)S(1)}, bf16[1,4,96,768]{3,2,1,0:T(8,128)(2,1)S(1)}, u32[]{:S(2)}, u32[]{:S(2)}) collective-permute-start(bf16[1,4,96,768]{3,2,1,0:T(8,128)(2,1)S(1)} %get-tuple-element.127), channel_id=1, source_target_pairs={{0,4},{1,5},{2,6},{3,7},{4,0},{5,1},{6,2},{7,3},{8,12},{9,13},{10,... | collective-permute-start | bytes 1769480 | tf_op jit(solution)/shard_map/ppermute | solution.py:605
  70.1 31.3 %collective-permute-start.10 = (bf16[2,2,96,768]{3,2,1,0:T(8,128)(2,1)}, bf16[2,2,96,768]{3,2,1,0:T(8,128)(2,1)}, u32[]{:S(2)}, u32[]{:S(2)}) collective-permute-start(bf16[2,2,96,768]{3,2,1,0:T(8,128)(2,1)} %pad_maximum_fusion.9), channel_id=1, source_target_pairs={{0,4},{1,5},{2,6},{3,7},{4,0},{5,1},{6,2},{7,3},{8,12},{9,13},{10,... | collective-permute-start | bytes 1769480 | tf_op jit(solution)/shard_map/ppermute | solution.py:605
  76.9 16.6 %collective-permute-start.7 = (bf16[2,2,96,768]{3,2,1,0:T(8,128)(2,1)}, bf16[2,2,96,768]{3,2,1,0:T(8,128)(2,1)}, u32[]{:S(2)}, u32[]{:S(2)}) collective-permute-start(bf16[2,2,96,768]{3,2,1,0:T(8,128)(2,1)} %pad_maximum_fusion.8), channel_id=1, source_target_pairs={{0,16},{1,17},{2,18},{3,19},{4,20},{5,21},{6,22},{7,23},{8,24},{9,... | collective-permute-start | bytes 1769480 | tf_op jit(solution)/shard_map/ppermute | solution.py:605
  82.0 40.9 %collective-permute-start.23 = (bf16[2,4,96,768]{3,2,1,0:T(8,128)(2,1)}, bf16[2,4,96,768]{3,2,1,0:T(8,128)(2,1)}, u32[]{:S(2)}, u32[]{:S(2)}) collective-permute-start(bf16[2,4,96,768]{3,2,1,0:T(8,128)(2,1)} %pad_maximum_fusion.6), channel_id=1, source_target_pairs={{0,4},{1,5},{2,6},{3,7},{4,0},{5,1},{6,2},{7,3},{8,12},{9,13},{10,... | collective-permute-start | bytes 3538952 | tf_op jit(solution)/shard_map/ppermute | solution.py:605
  89.9 37.1 %collective-permute-start.20 = (bf16[2,4,96,768]{3,2,1,0:T(8,128)(2,1)}, bf16[2,4,96,768]{3,2,1,0:T(8,128)(2,1)}, u32[]{:S(2)}, u32[]{:S(2)}) collective-permute-start(bf16[2,4,96,768]{3,2,1,0:T(8,128)(2,1)} %pad_maximum_fusion.5), channel_id=1, source_target_pairs={{0,16},{1,17},{2,18},{3,19},{4,20},{5,21},{6,22},{7,23},{8,24},{9,... | collective-permute-start | bytes 3538952 | tf_op jit(solution)/shard_map/ppermute | solution.py:605
  94.7 53.2 %collective-permute-start.8 = (bf16[4,2,96,768]{3,2,1,0:T(8,128)(2,1)S(1)}, bf16[4,2,96,768]{3,2,1,0:T(8,128)(2,1)}, u32[]{:S(2)}, u32[]{:S(2)}) collective-permute-start(bf16[4,2,96,768]{3,2,1,0:T(8,128)(2,1)S(1)} %pad_maximum_fusion.2.refs_5_), channel_id=1, source_target_pairs={{0,8},{1,9},{2,10},{3,11},{4,12},{5,13},{6,14},{7,15},{8,0},{9,1},... | collective-permute-start | bytes 3538952 | tf_op jit(solution)/shard_map/ppermute | solution.py:605
  102.7 45.2 %collective-permute-start.11 = (bf16[4,2,96,768]{3,2,1,0:T(8,128)(2,1)S(1)}, bf16[4,2,96,768]{3,2,1,0:T(8,128)(2,1)}, u32[]{:S(2)}, u32[]{:S(2)}) collective-permute-start(bf16[4,2,96,768]{3,2,1,0:T(8,128)(2,1)S(1)} %pad_maximum_fusion.3.refs_7_), channel_id=1, source_target_pairs={{0,8},{1,9},{2,10},{3,11},{4,12},{5,13},{6,14},{7,15},{8,0},{9,1},... | collective-permute-start | bytes 3538952 | tf_op jit(solution)/shard_map/ppermute | solution.py:605
  122.9 10.1 %collective-permute-start.1 = (bf16[128,768]{1,0:T(8,128)(2,1)}, bf16[128,768]{1,0:T(8,128)(2,1)S(1)}, u32[]{:S(2)}, u32[]{:S(2)}) collective-permute-start(bf16[128,768]{1,0:T(8,128)(2,1)} %get-tuple-element.141), channel_id=1, source_target_pairs={{0,1},{1,0},{2,3},{3,2},{4,9},{5,8},{6,11},{7,10},{8,5},{9,4},{10,... | collective-permute-start | bytes 589832 | tf_op jit(solution)/shard_map/ppermute | solution.py:605
  131.6 51.4 %collective-permute-start.21 = (bf16[4,4,96,768]{3,2,1,0:T(8,128)(2,1)}, bf16[4,4,96,768]{3,2,1,0:T(8,128)(2,1)}, u32[]{:S(2)}, u32[]{:S(2)}) collective-permute-start(bf16[4,4,96,768]{3,2,1,0:T(8,128)(2,1)} %pad_maximum_fusion.refs_7_), channel_id=1, source_target_pairs={{0,8},{1,9},{2,10},{3,11},{4,12},{5,13},{6,14},{7,15},{8,0},{9,1},... | collective-permute-start | bytes 7077896 | tf_op jit(solution)/shard_map/ppermute | solution.py:605
  133.7 49.3 %collective-permute-start.24 = (bf16[4,4,96,768]{3,2,1,0:T(8,128)(2,1)}, bf16[4,4,96,768]{3,2,1,0:T(8,128)(2,1)}, u32[]{:S(2)}, u32[]{:S(2)}) collective-permute-start(bf16[4,4,96,768]{3,2,1,0:T(8,128)(2,1)} %pad_maximum_fusion.1.refs_9_), channel_id=1, source_target_pairs={{0,8},{1,9},{2,10},{3,11},{4,12},{5,13},{6,14},{7,15},{8,0},{9,1},... | collective-permute-start | bytes 7077896 | tf_op jit(solution)/shard_map/ppermute | solution.py:605
  134.5 13.4 %collective-permute-start.2 = (bf16[128,768]{1,0:T(8,128)(2,1)}, bf16[128,768]{1,0:T(8,128)(2,1)S(1)}, u32[]{:S(2)}, u32[]{:S(2)}) collective-permute-start(bf16[128,768]{1,0:T(8,128)(2,1)} %get-tuple-element.143), channel_id=1, source_target_pairs={{0,2},{1,3},{2,0},{3,1},{4,10},{5,11},{6,8},{7,9},{8,6},{9,7},{10,... | collective-permute-start | bytes 589832 | tf_op jit(solution)/shard_map/ppermute | solution.py:605
  155.0 11.1 %collective-permute-start.12 = (bf16[2,512,768]{2,1,0:T(8,128)(2,1)S(1)}, bf16[2,512,768]{2,1,0:T(8,128)(2,1)S(1)}, u32[]{:S(2)}, u32[]{:S(2)}) collective-permute-start(bf16[2,512,768]{2,1,0:T(8,128)(2,1)S(1)} %get-tuple-element.72.own_ref), channel_id=1, source_target_pairs={{0,8},{1,9},{2,10},{3,11},{4,12},{5,13},{6,14},{7,15},{8,0},{9,1},... | collective-permute-start | bytes 4718600 | tf_op jit(solution)/shard_map/ppermute | solution.py:605
  155.5 9.7 %collective-permute-start.16 = (bf16[128,768]{1,0:T(8,128)(2,1)S(1)}, bf16[128,768]{1,0:T(8,128)(2,1)S(1)}, u32[]{:S(2)}, u32[]{:S(2)}) collective-permute-start(bf16[128,768]{1,0:T(8,128)(2,1)S(1)} %get-tuple-element.136), channel_id=1, source_target_pairs={{0,3},{1,2},{2,1},{3,0},{4,11},{5,10},{6,9},{7,8},{8,7},{9,6},{10,... | collective-permute-start | bytes 589832 | tf_op jit(solution)/shard_map/ppermute | solution.py:605
  158.0 24.9 %collective-permute-start.14 = (bf16[128,768]{1,0:T(8,128)(2,1)S(1)}, bf16[128,768]{1,0:T(8,128)(2,1)S(1)}, u32[]{:S(2)}, u32[]{:S(2)}) collective-permute-start(bf16[128,768]{1,0:T(8,128)(2,1)S(1)} %get-tuple-element.137), channel_id=1, source_target_pairs={{0,1},{1,0},{2,3},{3,2},{4,9},{5,8},{6,11},{7,10},{8,5},{9,4},{10,... | collective-permute-start | bytes 589832 | tf_op jit(solution)/shard_map/ppermute | solution.py:605
  165.3 17.7 %collective-permute-start.13 = (bf16[128,768]{1,0:T(8,128)(2,1)S(1)}, bf16[128,768]{1,0:T(8,128)(2,1)S(1)}, u32[]{:S(2)}, u32[]{:S(2)}) collective-permute-start(bf16[128,768]{1,0:T(8,128)(2,1)S(1)} %get-tuple-element.138), channel_id=1, source_target_pairs={{0,0},{1,1},{2,2},{3,3},{4,8},{5,9},{6,10},{7,11},{8,4},{9,5},{10,... | collective-permute-start | bytes 589832 | tf_op jit(solution)/shard_map/ppermute | solution.py:605
  166.1 16.8 %collective-permute-start.15 = (bf16[128,768]{1,0:T(8,128)(2,1)S(1)}, bf16[128,768]{1,0:T(8,128)(2,1)S(1)}, u32[]{:S(2)}, u32[]{:S(2)}) collective-permute-start(bf16[128,768]{1,0:T(8,128)(2,1)S(1)} %get-tuple-element.139), channel_id=1, source_target_pairs={{0,2},{1,3},{2,0},{3,1},{4,10},{5,11},{6,8},{7,9},{8,6},{9,7},{10,... | collective-permute-start | bytes 589832 | tf_op jit(solution)/shard_map/ppermute | solution.py:605
  206.1 57.3 %collective-permute-start.28 = (bf16[128,768]{1,0:T(8,128)(2,1)}, bf16[128,768]{1,0:T(8,128)(2,1)}, u32[]{:S(2)}, u32[]{:S(2)}) collective-permute-start(bf16[128,768]{1,0:T(8,128)(2,1)} %get-tuple-element.132), channel_id=1, source_target_pairs={{0,3},{1,2},{2,1},{3,0},{4,11},{5,10},{6,9},{7,8},{8,7},{9,6},{10,... | collective-permute-start | bytes 589832 | tf_op jit(solution)/shard_map/ppermute | solution.py:605
  208.1 62.4 %collective-permute-start.27 = (bf16[128,768]{1,0:T(8,128)(2,1)}, bf16[128,768]{1,0:T(8,128)(2,1)}, u32[]{:S(2)}, u32[]{:S(2)}) collective-permute-start(bf16[128,768]{1,0:T(8,128)(2,1)} %get-tuple-element.133), channel_id=1, source_target_pairs={{0,2},{1,3},{2,0},{3,1},{4,10},{5,11},{6,8},{7,9},{8,6},{9,7},{10,... | collective-permute-start | bytes 589832 | tf_op jit(solution)/shard_map/ppermute | solution.py:605
  234.5 7.8 %collective-permute-start.29 = (bf16[2,512,768]{2,1,0:T(8,128)(2,1)}, bf16[2,512,768]{2,1,0:T(8,128)(2,1)}, u32[]{:S(2)}, u32[]{:S(2)}) collective-permute-start(bf16[2,512,768]{2,1,0:T(8,128)(2,1)} %get-tuple-element.85), channel_id=1, source_target_pairs={{0,8},{1,9},{2,10},{3,11},{4,12},{5,13},{6,14},{7,15},{8,0},{9,1},... | collective-permute-start | bytes 4718600 | tf_op jit(solution)/shard_map/ppermute | solution.py:605
  239.1 70.1 %collective-permute-start.42 = (bf16[4,4,96,768]{3,2,1,0:T(8,128)(2,1)}, bf16[4,4,96,768]{3,2,1,0:T(8,128)(2,1)}, u32[]{:S(2)}, u32[]{:S(2)}) collective-permute-start(bf16[4,4,96,768]{3,2,1,0:T(8,128)(2,1)} %get-tuple-element.98), channel_id=1, source_target_pairs={{0,8},{1,9},{2,10},{3,11},{4,12},{5,13},{6,14},{7,15},{8,0},{9,1},... | collective-permute-start | bytes 7077896 | tf_op jit(solution)/shard_map/ppermute | solution.py:605
  240.1 71.5 %collective-permute-start.43 = (bf16[4,4,96,768]{3,2,1,0:T(8,128)(2,1)}, bf16[4,4,96,768]{3,2,1,0:T(8,128)(2,1)}, u32[]{:S(2)}, u32[]{:S(2)}) collective-permute-start(bf16[4,4,96,768]{3,2,1,0:T(8,128)(2,1)} %get-tuple-element.99), channel_id=1, source_target_pairs={{0,8},{1,9},{2,10},{3,11},{4,12},{5,13},{6,14},{7,15},{8,0},{9,1},... | collective-permute-start | bytes 7077896 | tf_op jit(solution)/shard_map/ppermute | solution.py:605
  263.5 9.2 %collective-permute-start.26 = (bf16[128,768]{1,0:T(8,128)(2,1)}, bf16[128,768]{1,0:T(8,128)(2,1)S(1)}, u32[]{:S(2)}, u32[]{:S(2)}) collective-permute-start(bf16[128,768]{1,0:T(8,128)(2,1)} %get-tuple-element.134), channel_id=1, source_target_pairs={{0,1},{1,0},{2,3},{3,2},{4,9},{5,8},{6,11},{7,10},{8,5},{9,4},{10,... | collective-permute-start | bytes 589832 | tf_op jit(solution)/shard_map/ppermute | solution.py:605
  275.4 23.6 %collective-permute-start.33 = (bf16[128,768]{1,0:T(8,128)(2,1)S(1)}, bf16[128,768]{1,0:T(8,128)(2,1)S(1)}, u32[]{:S(2)}, u32[]{:S(2)}) collective-permute-start(bf16[128,768]{1,0:T(8,128)(2,1)S(1)} %get-tuple-element.128), channel_id=1, source_target_pairs={{0,3},{1,2},{2,1},{3,0},{4,11},{5,10},{6,9},{7,8},{8,7},{9,6},{10,... | collective-permute-start | bytes 589832 | tf_op jit(solution)/shard_map/ppermute | solution.py:605
  278.1 21.3 %collective-permute-start.32 = (bf16[128,768]{1,0:T(8,128)(2,1)S(1)}, bf16[128,768]{1,0:T(8,128)(2,1)S(1)}, u32[]{:S(2)}, u32[]{:S(2)}) collective-permute-start(bf16[128,768]{1,0:T(8,128)(2,1)S(1)} %get-tuple-element.129), channel_id=1, source_target_pairs={{0,2},{1,3},{2,0},{3,1},{4,10},{5,11},{6,8},{7,9},{8,6},{9,7},{10,... | collective-permute-start | bytes 589832 | tf_op jit(solution)/shard_map/ppermute | solution.py:605
  279.6 19.4 %collective-permute-start.54 = (f32[12,768]{1,0:T(8,128)S(1)}, f32[12,768]{1,0:T(8,128)S(1)}, u32[]{:S(2)}, u32[]{:S(2)}) collective-permute-start(f32[12,768]{1,0:T(8,128)S(1)} %add.167), channel_id=1, source_target_pairs={{0,2},{1,3},{2,0},{3,1},{4,6},{5,7},{6,4},{7,5},{8,10},{9,11},{10,... | collective-permute-start | bytes 110600 | tf_op jit(solution)/shard_map/ppermute | solution.py:605
  299.0 18.2 %collective-permute-start.34 = (bf16[4,2,96,768]{3,2,1,0:T(8,128)(2,1)S(1)}, bf16[4,2,96,768]{3,2,1,0:T(8,128)(2,1)S(1)}, u32[]{:S(2)}, u32[]{:S(2)}) collective-permute-start(bf16[4,2,96,768]{3,2,1,0:T(8,128)(2,1)S(1)} %copy-done.28), channel_id=1, source_target_pairs={{0,8},{1,9},{2,10},{3,11},{4,12},{5,13},{6,14},{7,15},{8,0},{9,1},... | collective-permute-start | bytes 3538952 | tf_op jit(solution)/shard_map/ppermute | solution.py:605
  299.4 8.0 %collective-permute-start.30 = (bf16[128,768]{1,0:T(8,128)(2,1)S(1)}, bf16[128,768]{1,0:T(8,128)(2,1)S(1)}, u32[]{:S(2)}, u32[]{:S(2)}) collective-permute-start(bf16[128,768]{1,0:T(8,128)(2,1)S(1)} %get-tuple-element.131), channel_id=1, source_target_pairs={{0,0},{1,1},{2,2},{3,3},{4,8},{5,9},{6,10},{7,11},{8,4},{9,5},{10,... | collective-permute-start | bytes 589832 | tf_op jit(solution)/shard_map/ppermute | solution.py:605
  306.7 11.9 %collective-permute-start.35 = (bf16[4,2,96,768]{3,2,1,0:T(8,128)(2,1)S(1)}, bf16[4,2,96,768]{3,2,1,0:T(8,128)(2,1)S(1)}, u32[]{:S(2)}, u32[]{:S(2)}) collective-permute-start(bf16[4,2,96,768]{3,2,1,0:T(8,128)(2,1)S(1)} %copy-done.26), channel_id=1, source_target_pairs={{0,8},{1,9},{2,10},{3,11},{4,12},{5,13},{6,14},{7,15},{8,0},{9,1},... | collective-permute-start | bytes 3538952 | tf_op jit(solution)/shard_map/ppermute | solution.py:605
  310.9 28.9 %collective-permute-start.44 = (bf16[2,4,96,768]{3,2,1,0:T(8,128)(2,1)S(1)}, bf16[2,4,96,768]{3,2,1,0:T(8,128)(2,1)S(1)}, u32[]{:S(2)}, u32[]{:S(2)}) collective-permute-start(bf16[2,4,96,768]{3,2,1,0:T(8,128)(2,1)S(1)} %add_convert_fusion.1), channel_id=1, source_target_pairs={{0,16},{1,17},{2,18},{3,19},{4,20},{5,21},{6,22},{7,23},{8,24},{9,... | collective-permute-start | bytes 3538952 | tf_op jit(solution)/shard_map/ppermute | solution.py:605
  313.2 29.4 %collective-permute-start.45 = (bf16[2,4,96,768]{3,2,1,0:T(8,128)(2,1)S(1)}, bf16[2,4,96,768]{3,2,1,0:T(8,128)(2,1)S(1)}, u32[]{:S(2)}, u32[]{:S(2)}) collective-permute-start(bf16[2,4,96,768]{3,2,1,0:T(8,128)(2,1)S(1)} %add_convert_fusion), channel_id=1, source_target_pairs={{0,4},{1,5},{2,6},{3,7},{4,0},{5,1},{6,2},{7,3},{8,12},{9,13},{10,... | collective-permute-start | bytes 3538952 | tf_op jit(solution)/shard_map/ppermute | solution.py:605
  317.4 35.1 %collective-permute-start.36 = (bf16[2,2,96,768]{3,2,1,0:T(8,128)(2,1)S(1)}, bf16[2,2,96,768]{3,2,1,0:T(8,128)(2,1)S(1)}, u32[]{:S(2)}, u32[]{:S(2)}) collective-permute-start(bf16[2,2,96,768]{3,2,1,0:T(8,128)(2,1)S(1)} %add_convert_fusion.6), channel_id=1, source_target_pairs={{0,16},{1,17},{2,18},{3,19},{4,20},{5,21},{6,22},{7,23},{8,24},{9,... | collective-permute-start | bytes 1769480 | tf_op jit(solution)/shard_map/ppermute | solution.py:605
  318.7 36.0 %collective-permute-start.37 = (bf16[2,2,96,768]{3,2,1,0:T(8,128)(2,1)S(1)}, bf16[2,2,96,768]{3,2,1,0:T(8,128)(2,1)S(1)}, u32[]{:S(2)}, u32[]{:S(2)}) collective-permute-start(bf16[2,2,96,768]{3,2,1,0:T(8,128)(2,1)S(1)} %add_convert_fusion.5), channel_id=1, source_target_pairs={{0,4},{1,5},{2,6},{3,7},{4,0},{5,1},{6,2},{7,3},{8,12},{9,13},{10,... | collective-permute-start | bytes 1769480 | tf_op jit(solution)/shard_map/ppermute | solution.py:605
  341.1 26.2 %collective-permute-start.46 = (bf16[1,4,96,768]{3,2,1,0:T(8,128)(2,1)S(1)}, bf16[1,4,96,768]{3,2,1,0:T(8,128)(2,1)S(1)}, u32[]{:S(2)}, u32[]{:S(2)}) collective-permute-start(bf16[1,4,96,768]{3,2,1,0:T(8,128)(2,1)S(1)} %add_convert_fusion.4), channel_id=1, source_target_pairs={{0,4},{1,5},{2,6},{3,7},{4,0},{5,1},{6,2},{7,3},{8,12},{9,13},{10,... | collective-permute-start | bytes 1769480 | tf_op jit(solution)/shard_map/ppermute | solution.py:605
  343.8 23.5 %collective-permute-start.47 = (bf16[1,4,96,768]{3,2,1,0:T(8,128)(2,1)S(1)}, bf16[1,4,96,768]{3,2,1,0:T(8,128)(2,1)S(1)}, u32[]{:S(2)}, u32[]{:S(2)}) collective-permute-start(bf16[1,4,96,768]{3,2,1,0:T(8,128)(2,1)S(1)} %add_convert_fusion.3), channel_id=1, source_target_pairs={{0,16},{1,17},{2,18},{3,19},{4,20},{5,21},{6,22},{7,23},{8,24},{9,... | collective-permute-start | bytes 1769480 | tf_op jit(solution)/shard_map/ppermute | solution.py:605
  352.6 20.3 %collective-permute-start.38 = (bf16[1,2,96,768]{3,2,1,0:T(8,128)(2,1)S(1)}, bf16[1,2,96,768]{3,2,1,0:T(8,128)(2,1)S(1)}, u32[]{:S(2)}, u32[]{:S(2)}) collective-permute-start(bf16[1,2,96,768]{3,2,1,0:T(8,128)(2,1)S(1)} %add_convert_fusion.10), channel_id=1, source_target_pairs={{0,4},{1,5},{2,6},{3,7},{4,0},{5,1},{6,2},{7,3},{8,12},{9,13},{10,... | collective-permute-start | bytes 884744 | tf_op jit(solution)/shard_map/ppermute | solution.py:605
  354.8 18.1 %collective-permute-start.39 = (bf16[1,2,96,768]{3,2,1,0:T(8,128)(2,1)S(1)}, bf16[1,2,96,768]{3,2,1,0:T(8,128)(2,1)S(1)}, u32[]{:S(2)}, u32[]{:S(2)}) collective-permute-start(bf16[1,2,96,768]{3,2,1,0:T(8,128)(2,1)S(1)} %add_convert_fusion.9), channel_id=1, source_target_pairs={{0,16},{1,17},{2,18},{3,19},{4,20},{5,21},{6,22},{7,23},{8,24},{9,... | collective-permute-start | bytes 884744 | tf_op jit(solution)/shard_map/ppermute | solution.py:605
  367.8 35.0 %collective-permute-start.48 = (bf16[2,2,96,768]{3,2,1,0:T(8,128)(2,1)S(1)}, bf16[2,2,96,768]{3,2,1,0:T(8,128)(2,1)S(1)}, u32[]{:S(2)}, u32[]{:S(2)}) collective-permute-start(bf16[2,2,96,768]{3,2,1,0:T(8,128)(2,1)S(1)} %add_convert_fusion.2), channel_id=1, source_target_pairs={{0,2},{1,3},{2,0},{3,1},{4,6},{5,7},{6,4},{7,5},{8,10},{9,11},{10,... | collective-permute-start | bytes 1769480 | tf_op jit(solution)/shard_map/ppermute | solution.py:605
  373.1 34.9 %collective-permute-start.40 = (bf16[4,96,384]{2,1,0:T(8,128)(2,1)S(1)}, bf16[4,96,384]{2,1,0:T(8,128)(2,1)S(1)}, u32[]{:S(2)}, u32[]{:S(2)}) collective-permute-start(bf16[4,96,384]{2,1,0:T(8,128)(2,1)S(1)} %add_convert_fusion.8), channel_id=1, source_target_pairs={{0,2},{1,3},{2,0},{3,1},{4,6},{5,7},{6,4},{7,5},{8,10},{9,11},{10,... | collective-permute-start | bytes 884744 | tf_op jit(solution)/shard_map/ppermute | solution.py:605
  403.0 17.8 %collective-permute-start.49 = (bf16[2,1,96,768]{3,2,1,0:T(8,128)(2,1)S(1)}, bf16[2,1,96,768]{3,2,1,0:T(8,128)(2,1)S(1)}, u32[]{:S(2)}, u32[]{:S(2)}) collective-permute-start(bf16[2,1,96,768]{3,2,1,0:T(8,128)(2,1)S(1)} %add_convert_fusion.7), channel_id=1, source_target_pairs={{0,1},{1,0},{2,3},{3,2},{4,5},{5,4},{6,7},{7,6},{8,9},{9,8},{10,11... | collective-permute-start | bytes 884744 | tf_op jit(solution)/shard_map/ppermute | solution.py:605
  408.4 9.9 %collective-permute-start.41 = (bf16[4,96,192]{2,1,0:T(8,128)(2,1)S(1)}, bf16[4,96,192]{2,1,0:T(8,128)(2,1)S(1)}, u32[]{:S(2)}, u32[]{:S(2)}) collective-permute-start(bf16[4,96,192]{2,1,0:T(8,128)(2,1)S(1)} %add_convert_fusion.11), channel_id=1, source_target_pairs={{0,1},{1,0},{2,3},{3,2},{4,5},{5,4},{6,7},{7,6},{8,9},{9,8},{10,11... | collective-permute-start | bytes 442376 | tf_op jit(solution)/shard_map/ppermute | solution.py:605
  (68 other events, 564.2 us)
where the time goes:
time: 425 us; the launch traced here: 424 us
  waiting for transfers between devices  227 us (53%)
  Pallas kernels  83.1 us (20%)
  starting transfers between devices  59.2 us (14%)
  local copies, waits for them, and re-layouts  28.2 us (7%)
  other arithmetic  24.7 us (6%)
    ppermute x55, waiting for transfers between devices, move(): return lax.ppermute(data, AXES, pairs)  227 us
    ppermute x55, starting transfers between devices, move(): return lax.ppermute(data, AXES, pairs)  59.2 us
    pallas_call x1, Pallas kernels, hidden_both(): call(lambda *refs: hidden_body(layout, *refs), (blocks,), [frames] + [who...  22.3 us
    pallas_call x1, Pallas kernels, attend_backward(): call(attend_backward_body, (pairs,), [block, both, both, block, block, pl...  20.5 us
    unnamed x123, local copies, waits for them, and re-layouts  18.1 us
    concatenate x8, other arithmetic, spread(): data = jnp.concatenate([data, grid.swap(data, axis, bit)], 0)  13.9 us
    pallas_call x1, Pallas kernels, attend_forward(): call(attend_forward_body, (pairs,), [block, both, both], [block, pl.Block...  13.8 us
  transfers between devices with their start and end apart: 55, of which 26 were waited for; matrix products, arithmetic and copies ran while one was open for 8% of the time, Pallas kernels for 14%

commit v1 on v0

--- a/solution.py
+++ b/solution.py
@@ -78,25 +78,56 @@
         kind = bf16 if self.rows % 16 == 0 else f32
         return pltpu.VMEM((self.total, width), kind)
 
-    def join(self, place, ctx_first, mine, theirs, plane, target):
-        for other, ref in enumerate((mine, theirs)):
+    def blocks(self, place, ctx_first, refs):
+        half = self.count // 2
+        for other in range(CORES):
             for j in range(self.count):
                 rows = pl.ds(self.offset(place, ctx_first, other, j), self.rows)
-                target[rows, :] = ref[j, plane].astype(target.dtype)
-
-    def cut(self, place, ctx_first, source, mine, theirs, plane):
-        for other, ref in enumerate((mine, theirs)):
-            for j in range(self.count):
-                rows = pl.ds(self.offset(place, ctx_first, other, j), self.rows)
-                ref[j, plane] = source[rows, :].astype(bf16)
+                yield rows, refs[2 * other + j // half], j % half
+
+    def join(self, place, ctx_first, refs, plane, target):
+        for rows, ref, j in self.blocks(place, ctx_first, refs):
+            target[rows, :] = ref[j, plane].astype(target.dtype)
+
+    def cut(self, place, ctx_first, source, refs, plane):
+        for rows, ref, j in self.blocks(place, ctx_first, refs):
+            ref[j, plane] = source[rows, :].astype(bf16)
+
+
+def mirror(j, count):
+    out, step = 0, 1
+    while step < count:
+        out = out * 2 + (j // step) % 2
+        step *= 2
+    return out
+
+
+def turn_row(z, row, count, back=False):
+    size = row.shape[1] // count
+    blocks = [row[:, j * size : (j + 1) * size] for j in range(count)]
+    out = row
+    for at in range(count):
+        source = [mirror(j ^ at, count) if back else at ^ mirror(j, count) for j in range(count)]
+        out = jnp.where(z == at, jnp.concatenate([blocks[j] for j in source], 1), out)
+    return out
 
 
 def whole(*shape):
     return pl.BlockSpec(shape, lambda i, s: (0,) * len(shape))
 
 
-def call(body, grid, in_specs, out_specs, out_shape, scratch, flops, trans, moved, mib):
-    return pl.pallas_call(
+IN_HBM = {
+    "hidden_both": range(1, 12),
+    "attend_backward": range(7),
+    "weigh": (0, 4, 5),
+    "finish": (1, 2, 3),
+    "update_ff": range(-6, 0),
+    "update_proj": range(-6, 0),
+}
+
+
+def call(body, name, grid, in_specs, out_specs, out_shape, scratch, flops, trans, moved, mib):
+    kernel = pl.pallas_call(
         body,
         grid_spec=pltpu.PrefetchScalarGridSpec(
             num_scalar_prefetch=1,
@@ -110,44 +141,55 @@
         cost_estimate=pl.CostEstimate(flops=flops, transcendentals=trans, bytes_accessed=moved),
     )
 
+    def run(place, *arrays):
+        stay = IN_HBM.get(name, ())
+        stay = [j % len(arrays) for j in stay]
+        arrays = [
+            pltpu.with_memory_space_constraint(each, pltpu.HBM) if j in stay else each
+            for j, each in enumerate(arrays)
+        ]
+        return kernel(place, *arrays)
+
+    return run
+
 
 def project_body(
-    layout, place, x0, x1, x2, x3, ma, ta, mb, tb, vec_ref, bias_ref, x_ref, h_ref, q_ref, kv_ref, w_ref, joined
+    layout, tensor, place, x_ref, *refs
 ):
-    count = x0.shape[0]
-    for j, ref in enumerate((x0, x1, x2, x3)):
-        rows = slice(j * count, (j + 1) * count)
-        x_ref[rows, :] = ref[...]
-        norm_out, _, _ = layer_norm(ref[...].astype(f32), vec_ref[0:1, :], vec_ref[1:2, :])
-        h_ref[rows, :] = norm_out.astype(bf16)
+    sets = refs[0:4], refs[4:8]
+    vec_ref, h_ref, q_ref, kv_ref, w_ref, joined = refs[8:]
+    bias_query = turn_row(place[3], vec_ref[2:3, :], tensor)
+    bias_value = turn_row(place[3], vec_ref[3:4, :], tensor)
+    norm_out, _, _ = layer_norm(x_ref[...].astype(f32), vec_ref[0:1, :], vec_ref[1:2, :])
+    h_ref[...] = norm_out.astype(bf16)
     for plane in range(4):
         first = plane < 2
-        layout.join(place, first, ma if first else mb, ta if first else tb, plane % 2, joined)
+        layout.join(place, first, sets[plane // 2], plane % 2, joined)
         weight = joined[...].astype(bf16)
         w_ref[plane] = weight
         if plane == 3:
             break
         out = dot(h_ref[...], weight, 1, 0)
         if plane == 0:
-            q_ref[...] = (out + bias_ref[0:1, :]).astype(bf16)
+            q_ref[...] = (out + bias_query).astype(bf16)
         elif plane == 1:
             kv_ref[0] = out.astype(bf16)
         else:
-            kv_ref[1] = (out + bias_ref[1:2, :]).astype(bf16)
-
-
-def project(layout, place, x_pieces, pieces, vectors, biases):
-    step, width = x_pieces[0].shape
-    rows = step * len(x_pieces)
+            kv_ref[1] = (out + bias_value).astype(bf16)
+
+
+def project(layout, tensor, place, x_low, pieces, vectors):
+    rows, width = x_low.shape
     frames = whole(rows, width)
     return call(
-        lambda *refs: project_body(layout, *refs),
+        lambda *refs: project_body(layout, tensor, *refs),
+        "project",
         (1,),
-        [whole(step, width)] * len(x_pieces)
-        + [whole(*pieces[0].shape)] * 4
-        + [whole(*vectors.shape), whole(*biases.shape)],
-        [frames, frames, frames, whole(2, rows, width), whole(4, width, width)],
-        [jax.ShapeDtypeStruct((rows, width), bf16)] * 3
+        [frames]
+        + [whole(*pieces[0].shape)] * 8
+        + [whole(*vectors.shape)],
+        [frames, frames, whole(2, rows, width), whole(4, width, width)],
+        [jax.ShapeDtypeStruct((rows, width), bf16)] * 2
         + [
             jax.ShapeDtypeStruct((2, rows, width), bf16),
             jax.ShapeDtypeStruct((4, width, width), bf16),
@@ -157,7 +199,7 @@
         0,
         16 * width * width + 10 * rows * width,
         32,
-    )(place, *x_pieces, *pieces, vectors, biases)
+    )(place, x_low, *pieces, vectors)
 
 
 def attend_forward_body(place, q_ref, own_ref, far_ref, o_ref, lse_ref):
@@ -193,6 +235,7 @@
     both = pl.BlockSpec((2, rows, 2 * HD), lambda i, s: (0, 0, i))
     return call(
         attend_forward_body,
+        "attend_forward",
         (pairs,),
         [block, both, both],
         [block, pl.BlockSpec((1, 2, rows), lambda i, s: (i, 0, 0))],
@@ -262,6 +305,7 @@
     both = pl.BlockSpec((2, rows, 2 * HD), lambda i, s: (0, 0, i))
     return call(
         attend_backward_body,
+        "attend_backward",
         (pairs,),
         [block, both, both, block, block, pl.BlockSpec((1, 2, rows), lambda i, s: (i, 0, 0))],
         [block, both, both, pl.BlockSpec((2, 2 * HD), lambda i, s: (0, i))],
@@ -306,6 +350,7 @@
     rows, width = x_low.shape
     return call(
         mix_body,
+        "mix",
         (rows // TILE,),
         [
             tiles(width),
@@ -339,6 +384,7 @@
     rows, width = residual.shape
     return call(
         unmix_body,
+        "unmix",
         (rows // TILE,),
         [
             tiles(width),
@@ -366,47 +412,26 @@
     layout,
     place,
     h_ref,
-    e0,
-    e1,
-    e2,
-    e3,
+    e_ref,
     x_ref,
-    ma,
-    ta,
-    mb,
-    tb,
-    c1_ref,
-    c2_ref,
-    e_ref,
-    out_ref,
-    dh_ref,
-    ga,
-    fa,
-    gb,
-    fb,
-    dc1_ref,
-    h_t,
-    e_t,
-    total,
-    up_ref,
-    down_ref,
-    grad_ref,
+    *refs,
 ):
+    up_in, down_in = refs[0:4], refs[4:8]
+    c1_ref, c2_ref = refs[8:10]
+    out_ref, dh_ref = refs[10:12]
+    up_out, down_out = refs[12:16], refs[16:20]
+    dc1_ref, h_t, e_t, total, up_ref, down_ref, grad_ref = refs[20:]
     step = pl.program_id(0)
 
     @pl.when(step == 0)
     def _():
-        count = e0.shape[0]
-        for j, ref in enumerate((e0, e1, e2, e3)):
-            rows = slice(j * count, (j + 1) * count)
-            e_ref[rows, :] = ref[...]
-            e_t[:, rows] = ref[...].T
+        e_t[...] = e_ref[...].T
         h_t[...] = h_ref[...].T
         total[...] = x_ref[...] + c2_ref[...]
         dh_ref[...] = jnp.zeros_like(dh_ref)
 
-    layout.join(place, True, ma, ta, 0, up_ref)
-    layout.join(place, False, mb, tb, 0, down_ref)
+    layout.join(place, True, up_in, 0, up_ref)
+    layout.join(place, False, down_in, 0, down_ref)
     up = up_ref[...].astype(bf16)
     down = down_ref[...].astype(bf16)
     pre_act = dot(h_ref[...], up, 1, 0) + c1_ref[0]
@@ -418,9 +443,9 @@
     dc1_ref[0] = jnp.sum(dpre, 0, keepdims=True)
     dpre_low = dpre.astype(bf16)
     grad_ref[...] = dot(e_t[...], hidden, 1, 0).astype(grad_ref.dtype)
-    layout.cut(place, False, grad_ref, gb, fb, 0)
+    layout.cut(place, False, grad_ref, down_out, 0)
     grad_ref[...] = dot(h_t[...], dpre_low, 1, 0).astype(grad_ref.dtype)
-    layout.cut(place, True, grad_ref, ga, fa, 0)
+    layout.cut(place, True, grad_ref, up_out, 0)
     dh_ref[...] += dot(dpre_low, up, 1, 1)
 
     @pl.when(step == pl.num_programs(0) - 1)
@@ -428,27 +453,24 @@
         out_ref[...] = total[...].astype(bf16)
 
 
-def hidden_both(layout, place, h_low, e_pieces, residual, pieces, c1_rows, c2_row):
+def hidden_both(layout, place, h_low, cot, residual, pieces, c1_rows, c2_row):
     rows, width = h_low.shape
     count, blocks, block_rows, units = pieces[0].shape
     frames = whole(rows, width)
     piece = pl.BlockSpec((count, 1, block_rows, units), lambda i, s: (0, i, 0, 0))
-    bias = pl.BlockSpec((1, 1, units), lambda i, s: (s[3] ^ i, 0, 0))
+    bias = pl.BlockSpec((1, 1, units), lambda i, s: (s[3] ^ mirror(i, blocks), 0, 0))
     return call(
         lambda *refs: hidden_body(layout, *refs),
+        "hidden_both",
         (blocks,),
-        [frames]
-        + [whole(*each.shape) for each in e_pieces]
-        + [frames]
-        + [piece] * 4
+        [frames, frames, frames]
+        + [piece] * 8
         + [bias, whole(1, width)],
-        [frames, frames, frames] + [piece] * 4 + [bias],
-        [
-            jax.ShapeDtypeStruct((rows, width), bf16),
-            jax.ShapeDtypeStruct((rows, width), bf16),
-            jax.ShapeDtypeStruct((rows, width), f32),
-        ]
-        + [jax.ShapeDtypeStruct(pieces[0].shape, bf16)] * 4
+        [frames, frames]
+        + [piece] * 8
+        + [bias],
+        [jax.ShapeDtypeStruct((rows, width), bf16), jax.ShapeDtypeStruct((rows, width), f32)]
+        + [jax.ShapeDtypeStruct(pieces[0].shape, bf16)] * 8
         + [jax.ShapeDtypeStruct((blocks, 1, units), f32)],
         [
             pltpu.VMEM((width, rows), bf16),
@@ -462,12 +484,13 @@
         2 * rows * units * blocks,
         8 * width * units * blocks + 14 * rows * width,
         46,
-    )(place, h_low, *e_pieces, residual, *pieces, c1_rows[:, None, :], c2_row[None])
+    )(place, h_low, cot, residual, *pieces, c1_rows[:, None, :], c2_row[None])
 
 
 def weigh_body(
-    layout, place, h_ref, dq_ref, dkeep_ref, din_ref, dx_ref, o_ref, d_ref, ga, fa, gb, fb, grad_ref
+    layout, place, h_ref, dq_ref, dkeep_ref, din_ref, dx_ref, o_ref, d_ref, *refs
 ):
+    sets, grad_ref = (refs[0:4], refs[4:8]), refs[8]
     h_t = h_ref[...].T
     for plane in range(4):
         if plane == 0:
@@ -480,20 +503,20 @@
         else:
             grad = dot(dx_ref[...].T, o_ref[...], 1, 0)
         grad_ref[...] = grad.astype(grad_ref.dtype)
-        first = plane < 2
-        layout.cut(place, first, grad_ref, ga if first else gb, fa if first else fb, plane % 2)
+        layout.cut(place, plane < 2, grad_ref, sets[plane // 2], plane % 2)
 
 
 def weigh(layout, place, h_low, dquery, dkeep, din, dx_low, context):
     rows, width = h_low.shape
     frames = whole(rows, width)
-    shape = (layout.count, 2, layout.rows, width)
+    shape = (layout.count // 2, 2, layout.rows, width)
     return call(
         lambda *refs: weigh_body(layout, *refs),
+        "weigh",
         (1,),
         [frames, frames, whole(2, rows, width), whole(2, rows, width), frames, frames],
-        [whole(3, rows, width)] + [whole(*shape)] * 4,
-        [jax.ShapeDtypeStruct((3, rows, width), bf16)] + [jax.ShapeDtypeStruct(shape, bf16)] * 4,
+        [whole(3, rows, width)] + [whole(*shape)] * 8,
+        [jax.ShapeDtypeStruct((3, rows, width), bf16)] + [jax.ShapeDtypeStruct(shape, bf16)] * 8,
         [layout.scratch(width)],
         8 * rows * width * width,
         0,
@@ -502,20 +525,29 @@
     )(place, h_low, dquery, dkeep, din, dx_low, context)
 
 
-def finish_body(place, d_ref, w_ref, x_ref, dx_ref, vec_ref, out_ref, sums_ref):
+def finish_body(tensor, place, d_ref, w_ref, x_ref, dx_ref, vec_ref, mid_ref, qv_ref, dc1_ref, *refs):
+    out_ref, sums_ref = refs
     dnorm = None
     for plane in range(3):
         dnorm = add_dot(dnorm, d_ref[plane], w_ref[plane], 1, 1)
     _, normed, inv_scale = layer_norm(x_ref[...].astype(f32), vec_ref[0:1, :], vec_ref[1:2, :])
     out = dx_ref[...] + norm_back(dnorm, normed, inv_scale, vec_ref[0:1, :])
     out_ref[...] = out.astype(bf16)
-    gather_sums(sums_ref, dnorm * normed, dnorm)
-
-
-def finish(place, dproj, weights, x_low, dresidual, vectors):
+    sums_ref[0:1, :] = jnp.sum(dnorm * normed, 0, keepdims=True)
+    sums_ref[1:2, :] = jnp.sum(dnorm, 0, keepdims=True)
+    for j in range(2):
+        sums_ref[2 + j : 3 + j, :] = turn_row(place[3], qv_ref[j : j + 1, :], tensor, True)
+    sums_ref[4:8, :] = mid_ref[...]
+    for j in range(dc1_ref.shape[0]):
+        sums_ref[8 + j : 9 + j, :] = dc1_ref[j]
+
+
+def finish(place, dproj, weights, x_low, dresidual, vectors, rows_in, tensor):
     rows, width = x_low.shape
+    part = (rows, width)
     return call(
-        finish_body,
+        lambda *refs: finish_body(tensor, *refs),
+        "finish",
         (rows // TILE,),
         [
             tiles(width, 3),
@@ -523,15 +555,16 @@
             tiles(width),
             tiles(width),
             whole(*vectors.shape),
-        ],
-        [tiles(width), whole(2, width)],
-        [jax.ShapeDtypeStruct((rows, width), bf16), jax.ShapeDtypeStruct((2, width), f32)],
+        ]
+        + [whole(*each.shape) for each in rows_in],
+        [whole(*part), whole(*vectors.shape)],
+        [jax.ShapeDtypeStruct(part, bf16)] + [jax.ShapeDtypeStruct(vectors.shape, f32)],
         [],
         6 * rows * width * width,
         0,
         6 * width * width + 14 * rows * width,
         28,
-    )(place, dproj, weights, x_low, dresidual, vectors)
+    )(place, dproj, weights, x_low, dresidual, vectors, *rows_in)
 
 
 def update(refs, gradient):
@@ -540,27 +573,93 @@
         ref[...] = values
 
 
-def update_ff_body(place, *refs):
-    terms, refs = refs[:-14], refs[-14:]
-    total = sum(term[...].astype(f32) for term in terms)
-    update(refs[0:3] + refs[6:10], total[0, 0])
-    update(refs[3:6] + refs[10:14], total[1, 0])
-
-
-def update_proj_body(place, *refs):
-    terms, refs = refs[:-14], refs[-14:]
-    total = sum(term[...].astype(f32) for term in terms)
-    update(refs[0:3] + refs[6:10], total[:3])
-    update(refs[3:6] + refs[10:14], total[3].T)
-
-
-def update_both(place, body, terms, first, second):
+def pick(ref, at):
+    values = ref[...]
+    return values.reshape(values.shape[len(at[0]) :])
+
+
+def specs_of(terms):
+    specs = []
+    for array, lead, rows in terms:
+        rest = array.shape[len(lead) :]
+        if rows is None:
+            index, block = 0, rest
+        else:
+            index, count = rows
+            block = (count,) + rest[1:]
+        shape = (1,) * len(lead) + block
+        at = tuple(lead) + (index,) + (0,) * (len(block) - 1)
+        specs.append(pl.BlockSpec(shape, lambda i, s, at=at: at))
+    return specs
+
+
+def merge(place, name, groups, columns=None):
+    terms = [term for group in groups for term in group]
+    shapes = []
+    for group in groups:
+        array, lead, rows = group[0]
+        shape = array.shape[len(lead) :]
+        shape = shape if rows is None else (rows[1],) + shape[1:]
+        shapes.append(shape if columns is None else shape[:-1] + (columns.stop - columns.start,))
+    stacked = columns is None
+    out = (len(groups),) + shapes[0] if stacked else (sum(x[0] for x in shapes),) + shapes[0][1:]
+
+    def body(place, *refs):
+        out_ref, refs = refs[-1], list(refs[:-1])
+        first = 0
+        for g, group in enumerate(groups):
+            total = None
+            for _, lead, _ in group:
+                values = pick(refs.pop(0), (lead, None)).astype(f32)
+                if columns is not None and values.shape[-1] > shapes[g][-1]:
+                    values = values[..., columns]
+                total = values if total is None else total + values
+            if stacked:
+                out_ref[g] = total.astype(bf16)
+            else:
+                out_ref[first : first + shapes[g][0]] = total.astype(bf16)
+            first += shapes[g][0]
+
+    return call(
+        body,
+        name,
+        (1,),
+        specs_of(terms),
+        whole(*out),
+        jax.ShapeDtypeStruct(out, bf16),
+        [],
+        0,
+        0,
+        4 * len(terms) * shapes[0][-1] * shapes[0][-2],
+        16,
+    )(place, *[array for array, _, _ in terms])
+
+
+def update_both(place, name, groups, columns, split, first, second):
+    terms = [term for group in groups for term in group]
     shapes = [first[0].shape] * 4 + [second[0].shape] * 4
-    inputs = list(terms) + list(first) + list(second)
+    states = list(first) + list(second)
+
+    def body(place, *refs):
+        refs = list(refs)
+        sums = []
+        for group in groups:
+            total = None
+            for _, lead, _ in group:
+                values = pick(refs.pop(0), (lead, None)).astype(f32)
+                if columns is not None and values.shape[-1] > columns:
+                    values = values[..., :columns]
+                total = values if total is None else total + values
+            sums.append(total)
+        grads = split(*sums)
+        update(refs[0:3] + refs[6:10], grads[0])
+        update(refs[3:6] + refs[10:14], grads[1])
+
     out = call(
         body,
+        name,
         (1,),
-        [whole(*each.shape) for each in inputs],
+        specs_of(terms) + [whole(*each.shape) for each in states],
         [whole(*shape) for shape in shapes],
         [jax.ShapeDtypeStruct(shape, f32) for shape in shapes],
         [],
@@ -568,7 +667,7 @@
         first[0].size + second[0].size,
         32 * (first[0].size + second[0].size),
         20,
-    )(place, *inputs)
+    )(place, *[array for array, _, _ in terms], *states)
     return out[:4], out[4:]
 
 
@@ -608,17 +707,10 @@
         dim = ("x", "core", "y", "z").index(axis)
         return self.move(data, lambda *at: tuple(v ^ bit if i == dim else v for i, v in enumerate(at)))
 
-    def turn(self, rows):
-        for bit in bits(self.tensor):
-            order = [j ^ bit for j in range(self.tensor)]
-            other = jnp.stack([rows[j] for j in order])
-            rows = jnp.where((self.z & bit) != 0, other, rows)
-        return rows
-
 
 def over_tensor(grid, shard):
     data = shard[None]
-    for bit in bits(grid.tensor):
+    for bit in reversed(list(bits(grid.tensor))):
         data = jnp.concatenate([data, grid.swap(data, "z", bit)], 0)
     return data
 
@@ -630,31 +722,36 @@
 
 
 def spread(grid, planes, ctx_first):
-    data = planes[None]
+    data, high = None, planes[None]
     for axis, bit in axis_bits(grid, ctx_first):
-        data = jnp.concatenate([data, grid.swap(data, axis, bit)], 0)
-    return data, grid.swap(data, "core")
-
-
-def collect(grid, keep, give, ctx_first):
-    terms = [keep, grid.swap(give, "core")]
-    for axis, bit in reversed(axis_bits(grid, ctx_first)):
-        half = terms[0].shape[0] // 2
-        out = sum(term[half:].astype(f32) for term in terms).astype(bf16)
-        terms = [term[:half] for term in terms] + [grid.swap(out, axis, bit)]
-    return [term[0] for term in terms]
+        data = high if data is None else jnp.concatenate([data, high], 0)
+        high = grid.swap(data, axis, bit)
+    far_low = grid.swap(data, "core")
+    far_high = grid.swap(high, "core")
+    return data, high, far_low, far_high
+
+
+def collect(grid, parts, ctx_first):
+    low, high, give_low, give_high = parts
+    high_terms = [high, grid.swap(give_high, "core")]
+    terms = [low, grid.swap(give_low, "core")]
+    for step, (axis, bit) in enumerate(reversed(axis_bits(grid, ctx_first))):
+        if step > 0:
+            half = len_of(terms) // 2
+            high_terms = [term[half : 2 * half] for term in terms]
+        out = total_of(high_terms).astype(bf16)
+        if step > 0:
+            terms = list(terms)
+        terms = terms + [grid.swap(out, axis, bit)]
+    return [(term, (0,)) for term in terms]
+
+
+def len_of(terms):
+    return min(term.shape[0] for term in terms)
 
 
 def total_of(terms):
     return sum(term.astype(f32) for term in terms)
-
-
-def to_owner(grid, terms, split):
-    for bit in reversed(list(bits(grid.tensor))):
-        halves = [split(term, bit) for term in terms]
-        out = total_of([half[1] for half in halves]).astype(bf16)
-        terms = [half[0] for half in halves] + [grid.swap(out, "z", bit)]
-    return terms
 
 
 def sum_everywhere(grid, rows):
@@ -665,39 +762,53 @@
     return rows
 
 
+def cross(grid, data):
+    return grid.move(data, lambda f, c, y, z: (f, y, c, z))
+
+
 def clips_in(grid, frames):
-    pieces = []
-    for j in range(grid.tensor):
-        out = lax.dynamic_index_in_dim(frames, grid.z ^ j, 0, False)
-        pieces.append(grid.move(out, lambda f, c, y, z: (f, y, c, z ^ j)))
-    return pieces
-
-
-def clips_out_body(place, *refs):
-    out_ref = refs[-1]
-    for j, ref in enumerate(refs[:-1]):
-        out_ref[pl.ds(place[3] ^ j, 1)] = ref[...].astype(out_ref.dtype)[None]
-
-
-def clips_out(grid, rows, kind):
-    step = rows.shape[0] // grid.tensor
-    pieces = []
-    for j in range(grid.tensor):
-        out = rows[j * step : (j + 1) * step]
-        pieces.append(grid.move(out, lambda f, c, y, z: (f, y, c, z ^ j)))
-    shape = (step, rows.shape[1])
+    frames = cross(grid, frames)
+
+    def clip(j):
+        return lax.dynamic_index_in_dim(frames, grid.z ^ j, 0, True)
+
+    two = grid.swap(jnp.concatenate([clip(2), clip(3)], 0), "z", 2)
+    one = grid.swap(jnp.concatenate([clip(1), two[1:]], 0), "z", 1)
+    data = jnp.concatenate([clip(0), two[:1], one], 0)
+    return data.reshape(-1, data.shape[-1])
+
+
+def clips_out(grid, rows, kind, name, early):
+    data = rows.reshape(grid.tensor, -1, rows.shape[-1])
+    if early:
+        data = cross(grid, data)
+    one = grid.swap(data[2:], "z", 1)
+    two = grid.swap(jnp.concatenate([data[1:2], one[1:]], 0), "z", 2)
+    parts = [data[:1], one[:1], two]
+    if not early:
+        parts = [cross(grid, jnp.concatenate(parts, 0))]
+
+    def body(place, *refs):
+        j = 0
+        for ref in refs[:-1]:
+            for row in range(ref.shape[0]):
+                refs[-1][pl.ds(place[3] ^ j, 1)] = ref[row : row + 1].astype(kind)
+                j += 1
+
+    first = [each.shape if len(parts) == 1 else (min(each.shape[0], 2),) + each.shape[1:] for each in parts]
     return call(
-        clips_out_body,
+        body,
+        name,
         (1,),
-        [whole(*shape)] * grid.tensor,
-        whole(grid.tensor, *shape),
-        jax.ShapeDtypeStruct((grid.tensor,) + shape, kind),
+        [whole(*shape) for shape in first],
+        whole(*data.shape),
+        jax.ShapeDtypeStruct(data.shape, kind),
         [],
         0,
         0,
-        8 * rows.size,
+        8 * data.size,
         10,
-    )(grid.place, *pieces)
+    )(grid.place, *parts)
 
 
 def step_of(
@@ -721,37 +832,31 @@
 ):
     grid = Grid()
     place = grid.place
-    width = frames_in.shape[2]
     part = attend_weight.shape[2]
     layout = Layout(grid.outer, grid.ctx, up_weight.shape[0])
 
     shard = jnp.concatenate([attend_weight.astype(bf16), output_weight.astype(bf16).T[None]], 0)
     proj = over_tensor(grid, shard)
     proj = jnp.concatenate([proj[j] for j in range(grid.tensor)], 2)
-    x_pieces = clips_in(grid, frames_in)
+    x_low = clips_in(grid, frames_in)
     proj_pieces = spread(grid, proj[:2], True) + spread(grid, proj[2:], False)
     shard = jnp.stack([up_weight.astype(bf16), down_weight.astype(bf16).T])
     ff = over_tensor(grid, shard)
     ff_pieces = spread(grid, ff[:, 0], True) + spread(grid, ff[:, 1], False)
-    e_pieces = clips_in(grid, out_cotangent)
-
-    def turned(row):
-        return grid.turn(row.reshape(grid.tensor, part)).reshape(1, width)
-
-    biases = jnp.concatenate([turned(vectors[2]), turned(vectors[3])], 0)
-
-    x_low, in_norm1, queries, own, weights = project(
-        layout, place, x_pieces, proj_pieces, vectors, biases
+    cot_low = clips_in(grid, out_cotangent)
+
+    in_norm1, queries, own, weights = project(
+        layout, grid.tensor, place, x_low, proj_pieces, vectors
     )
     far = grid.swap(own, "core")
     context, log_total = attend_forward(place, queries, own, far)
     residual, in_norm2 = mix(place, x_low, context, weights, vectors)
-    cot_low, result, dnorm2, ga, fa, gb, fb, grad_c1 = hidden_both(
-        layout, place, in_norm2, e_pieces, residual, ff_pieces, vectors[8:12], vectors[7]
-    )
-    frames_out = clips_out(grid, result, bf16)
-    ff_a = collect(grid, ga, fa, True)
-    ff_b = collect(grid, gb, fb, False)
+    result, dnorm2, *grads, grad_c1 = hidden_both(
+        layout, place, in_norm2, cot_low, residual, ff_pieces, vectors[8:12], vectors[7]
+    )
+    ff_a = collect(grid, grads[:4], True)
+    ff_b = collect(grid, grads[4:], False)
+    frames_out = clips_out(grid, result, bf16, "y_out", False)
 
     dresidual, dres_low, dcontext, mid_sums = unmix(
         place, dnorm2, residual, cot_low, weights, vectors
@@ -760,39 +865,63 @@
         place, queries, own, far, context, dcontext, log_total
     )
     din = grid.swap(dgive, "core")
-    dproj, ga, fa, gb, fb = weigh(layout, place, in_norm1, dquery, dkeep, din, dres_low, context)
-    proj_a = collect(grid, ga, fa, True)
-    proj_b = collect(grid, gb, fb, False)
-    dinputs, end_sums = finish(place, dproj, weights, x_low, dresidual, vectors)
-    frames_grad = clips_out(grid, dinputs, f32)
-
-    vector_part = jnp.concatenate(
-        [end_sums, jnp.stack([turned(sums[0])[0], turned(sums[1])[0]]), mid_sums, grad_c1[:, 0, :]],
-        0,
-    )
+    dproj, *grads = weigh(layout, place, in_norm1, dquery, dkeep, din, dres_low, context)
+    proj_a = collect(grid, grads[:4], True)
+    proj_b = collect(grid, grads[4:], False)
+    dinputs, vector_part = finish(
+        place, dproj, weights, x_low, dresidual, vectors, [mid_sums, sums, grad_c1], grid.tensor
+    )
+    frames_grad = clips_out(grid, dinputs, f32, "dx_out", True)
     vector_grad = sum_everywhere(grid, vector_part)
 
-    def by_block(term, bit):
-        return term[:, :bit], term[:, bit:]
-
-    def by_column(term, bit):
-        return term[..., : bit * part], term[..., bit * part :]
-
-    terms = to_owner(grid, [jnp.stack(pair) for pair in zip(ff_a, ff_b)], by_block)
+    groups = [ff_a, ff_b]
+    arrived = []
+    count = grid.tensor
+    for bit in bits(grid.tensor):
+        count //= 2
+        name = f"gff_z{bit}"
+        send = [[(a, at, (1, count)) for a, at in group] for group in groups]
+        for a, _ in arrived:
+            for g, group in enumerate(send):
+                group.append((a, (g,), (1, count)))
+        data = merge(place, name, send)
+        arrived.append((grid.swap(data, "z", bit), None))
+    terms = [[(a, at, (0, 1)) for a, at in group] for group in groups]
+    for g, group in enumerate(terms):
+        group += [(a, (g,), (0, 1)) for a, _ in arrived]
     ups, downs = update_both(
         place,
-        update_ff_body,
+        "update_ff",
         terms,
+        None,
+        lambda up, down: (up[0], down[0]),
         (up_weight, up_mean, up_square),
         (down_weight.T, down_mean.T, down_square.T),
     )
     up_grad, up_new, up_mean_new, up_square_new = ups
     down_grad, down_new, down_mean_new, down_square_new = [each.T for each in downs]
-    terms = to_owner(grid, [jnp.concatenate(pair, 0) for pair in zip(proj_a, proj_b)], by_column)
+
+    groups = [proj_a, proj_b]
+    arrived = []
+    count = grid.tensor
+    for bit in bits(grid.tensor):
+        count //= 2
+        name = f"gproj_z{bit}"
+        send = [[(a, at, None) for a, at in group] for group in groups]
+        for a in arrived:
+            for g, group in enumerate(send):
+                group.append((a, (), (g, 2)))
+        data = merge(place, name, send, slice(count * part, 2 * count * part))
+        arrived.append(grid.swap(data, "z", bit))
+    terms = [[(a, at, None) for a, at in group] for group in groups]
+    for g, group in enumerate(terms):
+        group += [(a, (), (g, 2)) for a in arrived]
     attends, outputs = update_both(
         place,
-        update_proj_body,
+        "update_proj",
         terms,
+        part,
+        lambda one, two: (jnp.concatenate([one, two[:1]], 0), two[1].T),
         (attend_weight, attend_mean, attend_square),
         (output_weight, output_mean, output_square),
     )

time: 425 us -> 340 us (0.80)
  waiting for transfers between devices: 227 us -> 143 us
  starting transfers between devices: 59.2 us -> 74.1 us
  other arithmetic: 24.7 us -> 13.2 us
  local copies, waits for them, and re-layouts: 28.2 us -> 17 us
  Pallas kernels: 83.1 us -> 90.2 us
    ppermute x55 -> x59, waiting for transfers between devices: 227 us -> 143 us  [move(): return lax.ppermute(data, AXES, pairs)]
    ppermute x55 -> x59, starting transfers between devices: 59.2 us -> 74.1 us  [move(): return lax.ppermute(data, AXES, pairs)]
    pallas_call x12 -> x16, Pallas kernels: 83.1 us -> 90.2 us  [run(): return kernel(place, *arrays)]
    concatenate x13, other arithmetic: 13.9 us -> 7.26 us  [the longest x4 3.09 us: spread(): data = high if data is None else jnp.concatenate([data, high], 0)]
    unnamed x123 -> x81, local copies, waits for them, and re-layouts: 18.1 us -> 11.7 us
    convert_element_type x12 -> x8, other arithmetic: 7.47 us -> 1.56 us  [collect(): out = total_of(high_terms).astype(bf16)]
    slice x19 -> x9, local copies, waits for them, and re-layouts: 5.7 us -> 1.24 us  [the longest x2 1.07 us: clips_in(): data = jnp.concatenate([clip(0), two[:1], one], 0)]
  transfers between devices with their start and end apart: 55 -> 59, of which waited for: 26 -> 23; matrix products, arithmetic and copies ran while one was open for 8% -> 5% of each run, Pallas kernels for 14% -> 12%
where the time goes in v1:
time: 340 us; the launch traced here: 339 us
  waiting for transfers between devices  143 us (42%)
  Pallas kernels  90.2 us (27%)
  starting transfers between devices  74.1 us (22%)
  local copies, waits for them, and re-layouts  17 us (5%)
  other arithmetic  13.2 us (4%)
    ppermute x59, waiting for transfers between devices, move(): return lax.ppermute(data, AXES, pairs)  143 us
    pallas_call x16, Pallas kernels, run(): return kernel(place, *arrays)  90.2 us
    ppermute x59, starting transfers between devices, move(): return lax.ppermute(data, AXES, pairs)  74.1 us
    unnamed x81, local copies, waits for them, and re-layouts  11.7 us
  transfers between devices with their start and end apart: 59, of which 23 were waited for; matrix products, arithmetic and copies ran while one was open for 5% of the time, Pallas kernels for 12%

profile of v1, /device:TPU:0, one launch (start us, length us, event | category | flops | bytes accessed | tf_op | source)
XLA Modules:
  0.0 338.7 jit_solution(10553058196020375016)
XLA Ops:
  2.8 4.1 %collective-permute-start.3 = (bf16[1,4,96,192]{3,2,1,0:T(8,128)(2,1)S(1)}, bf16[1,4,96,192]{3,2,1,0:T(8,128)(2,1)S(1)}, u32[]{:S(2)}, u32[]{:S(2)}) collective-permute-start(bf16[1,4,96,192]{3,2,1,0:T(8,128)(2,1)S(1)} %maximum_bitcast_fusion.1), channel_id=1, source_target_pairs={{0,2},{1,3},{2,0},{3,1},{4,6},{5,7},{6,4},{7,5},{8,10},{9,11},{10,... | collective-permute-start | bytes 442376 | tf_op jit(solution)/shard_map/ppermute | solution.py:704
  6.9 9.1 %collective-permute-done.3 = bf16[1,4,96,192]{3,2,1,0:T(8,128)(2,1)S(1)} collective-permute-done((bf16[1,4,96,192]{3,2,1,0:T(8,128)(2,1)S(1)}, bf16[1,4,96,192]{3,2,1,0:T(8,128)(2,1)S(1)}, u32[]{:S(2)}, u32[]{:S(2)}) %collective-permute-start.3) | collective-permute-done | bytes 147488 | tf_op jit(solution)/shard_map/ppermute | solution.py:704
  16.9 3.4 %collective-permute-start.17 = (bf16[1,2,96,768]{3,2,0,1:T(8,128)(2,1)S(1)}, bf16[1,2,96,768]{3,2,0,1:T(8,128)(2,1)S(1)}, u32[]{:S(2)}, u32[]{:S(2)}) collective-permute-start(bf16[1,2,96,768]{3,2,0,1:T(8,128)(2,1)S(1)} %maximum_bitcast_fusion), channel_id=1, source_target_pairs={{0,2},{1,3},{2,0},{3,1},{4,6},{5,7},{6,4},{7,5},{8,10},{9,11},{10,... | collective-permute-start | bytes 884744 | tf_op jit(solution)/shard_map/ppermute | solution.py:704
  20.4 7.4 %collective-permute-start = (bf16[4,128,768]{2,1,0:T(8,128)(2,1)}, bf16[4,128,768]{2,1,0:T(8,128)(2,1)}, u32[]{:S(2)}, u32[]{:S(2)}) collective-permute-start(bf16[4,128,768]{2,1,0:T(8,128)(2,1)} %param.19), channel_id=1, source_target_pairs={{0,0},{1,1},{2,2},{3,3},{4,8},{5,9},{6,10},{7,11},{8,4},{9,5},{10,... | collective-permute-start | bytes 2359304 | tf_op jit(solution)/shard_map/ppermute | solution.py:704
  27.8 7.4 %collective-permute-start.14 = (bf16[4,128,768]{2,1,0:T(8,128)(2,1)}, bf16[4,128,768]{2,1,0:T(8,128)(2,1)}, u32[]{:S(2)}, u32[]{:S(2)}) collective-permute-start(bf16[4,128,768]{2,1,0:T(8,128)(2,1)} %param.20), channel_id=1, source_target_pairs={{0,0},{1,1},{2,2},{3,3},{4,8},{5,9},{6,10},{7,11},{8,4},{9,5},{10,... | collective-permute-start | bytes 2359304 | tf_op jit(solution)/shard_map/ppermute | solution.py:704
  35.6 1.6 collective-permute-start.9
  38.1 10.6 %collective-permute-done.5 = bf16[1,2,96,768]{3,2,1,0:T(8,128)(2,1)S(1)} collective-permute-done((bf16[1,2,96,768]{3,2,1,0:T(8,128)(2,1)S(1)}, bf16[1,2,96,768]{3,2,1,0:T(8,128)(2,1)S(1)}, u32[]{:S(2)}, u32[]{:S(2)}) %collective-permute-start.5) | collective-permute-done | bytes 294944 | tf_op jit(solution)/shard_map/ppermute | solution.py:704
  48.8 1.6 collective-permute-start.6
  50.5 2.5 constant_dynamic-slice_fusion.3
  56.6 1.8 collective-permute-start.19
  58.4 16.4 %collective-permute-done.1 = bf16[2,128,768]{2,1,0:T(8,128)(2,1)} collective-permute-done((bf16[2,128,768]{2,1,0:T(8,128)(2,1)}, bf16[2,128,768]{2,1,0:T(8,128)(2,1)}, u32[]{:S(2)}, u32[]{:S(2)}) %collective-permute-start.1) | collective-permute-done | bytes 393248 | tf_op jit(solution)/shard_map/ppermute | solution.py:704
  80.7 1.6 pad_maximum_fusion.1.refs_4_
  84.2 6.2 %collective-permute-done.2 = bf16[2,128,768]{2,1,0:T(8,128)(2,1)S(1)} collective-permute-done((bf16[2,128,768]{2,1,0:T(8,128)(2,1)S(1)}, bf16[2,128,768]{2,1,0:T(8,128)(2,1)S(1)}, u32[]{:S(2)}, u32[]{:S(2)}) %collective-permute-start.2) | collective-permute-done | bytes 393248 | tf_op jit(solution)/shard_map/ppermute | solution.py:704
  91.3 3.1 shard_map.354
  95.3 7.7 %collective-permute-done.15 = bf16[2,128,768]{2,1,0:T(8,128)(2,1)S(1)} collective-permute-done((bf16[2,128,768]{2,1,0:T(8,128)(2,1)S(1)}, bf16[2,128,768]{2,1,0:T(8,128)(2,1)S(1)}, u32[]{:S(2)}, u32[]{:S(2)}) %collective-permute-start.15) | collective-permute-done | bytes 393248 | tf_op jit(solution)/shard_map/ppermute | solution.py:704
  103.3 10.3 %collective-permute-done.16 = bf16[2,128,768]{2,1,0:T(8,128)(2,1)S(1)} collective-permute-done((bf16[2,128,768]{2,1,0:T(8,128)(2,1)S(1)}, bf16[2,128,768]{2,1,0:T(8,128)(2,1)S(1)}, u32[]{:S(2)}, u32[]{:S(2)}) %collective-permute-start.16) | collective-permute-done | bytes 393248 | tf_op jit(solution)/shard_map/ppermute | solution.py:704
  114.1 3.5 %collective-permute-done.24.refs_9_ = bf16[2,4,96,768]{3,2,1,0:T(8,128)(2,1)S(1)} collective-permute-done((bf16[2,4,96,768]{3,2,1,0:T(8,128)(2,1)S(1)}, bf16[2,4,96,768]{3,2,1,0:T(8,128)(2,1)S(1)}, u32[]{:S(2)}, u32[]{:S(2)}) %collective-permute-start.24) | collective-permute-done | bytes 1179680 | tf_op jit(solution)/shard_map/ppermute | solution.py:704
  119.3 14.0 %shard_map.355 = (bf16[512,768]{1,0:T(8,128)(2,1)S(1)}, f32[6,2,512]{2,1,0:T(2,128)S(1)}) custom-call(s32[4]{0:T(128)S(1)} %fusion.1.refs_0_.place, bf16[512,768]{1,0:T(8,128)(2,1)S(1)} %get-tuple-element.76.q_ref, bf16[2,512,768]{2,1,0:T(8,128)(2,1)S(1)} %get-tuple-element.77.own_ref, bf16[2,512,768]{2,1,0:T(8,128)(2,1)S(1)} %collective-permute-done.13.far_ref), custom_call_target="tpu_custom_call" | custom-call | flops 1610612736 | bytes 4718592 | tf_op jit(solution)/shard_map/pallas_call | solution.py:151
  135.4 1.8 shard_map.356
  140.5 24.0 %shard_map.357 = (bf16[512,768]{1,0:T(8,128)(2,1)S(1)}, f32[512,768]{1,0:T(8,128)}, bf16[2,4,96,768]{3,2,1,0:T(8,128)(2,1)S(1)}, bf16[2,4,96,768]{3,2,1,0:T(8,12...) custom-call(s32[4]{0:T(128)S(1)} %fusion.1.refs_0_.place, ...), custom_call_target="tpu_custom_call" | custom-call | flops 14495514624 | bytes 24379392 | tf_op jit(solution)/shard_map/pallas_call | solution.py:151
  165.9 2.5 shard_map.359
  171.3 20.4 %shard_map.360 = (bf16[512,768]{1,0:T(8,128)(2,1)S(1)}, f32[2,512,768]{2,1,0:T(8,128)S(1)}, bf16[2,512,768]{2,1,0:T(8,128)(2,1)S(1)}, f32[2,768]{1,0:T(2,128)S(1)}) custom-call(s32[4]{0:T(128)S(1)} %fusion.1.refs_0_.place, bf16[512,768]{1,0:T(8,128)(2,1)} %copy-done.18, bf16[2,512,768]{2,1,0:T(8,128)(2,1)} %copy-done.9, bf16[2,512,768]{2,1,0:T(8,128)(2,1)} %copy-done.10, ...), custom_call_target="tpu_custom_call" | custom-call | flops 4026531840 | bytes 12582912 | tf_op jit(solution)/shard_map/pallas_call | solution.py:151
  193.0 2.2 collective-permute-done.30.refs_4_
  195.6 5.1 %shard_map.361 = (bf16[3,512,768]{2,1,0:T(8,128)(2,1)S(1)}, bf16[2,2,96,768]{3,2,1,0:T(8,128)(2,1)S(1)}, bf16[2,2,96,768]{3,2,1,0:T(8,128)(2,1)S(1)}, bf16[2,2,9...) custom-call(s32[4]{0:T(128)S(1)} %fusion.1.refs_0_.place, ...), custom_call_target="tpu_custom_call" | custom-call | flops 2415919104 | bytes 15728640 | tf_op jit(solution)/shard_map/pallas_call | solution.py:151
  201.3 6.0 %shard_map.362 = (bf16[512,768]{1,0:T(8,128)(2,1)S(1)}, f32[12,768]{1,0:T(8,128)S(1)}) custom-call(s32[4]{0:T(128)S(1)} %fusion.1.refs_0_.place, bf16[3,512,768]{2,1,0:T(8,128)(2,1)S(1)} %get-tuple-element.91.refs_1_, bf16[4,768,768]{2,1,0:T(8,128)(2,1)} %copy-done, bf16[512,768]{1,0:T(8,128)(2,1)} %bitcast.45, f32[512,768]{1,0:T(8,128)} %copy-done.3, ...), custom_call_target="tpu_custom_call" | custom-call | flops 1811939328 | bytes 9043968 | tf_op jit(solution)/shard_map/pallas_call | solution.py:151
  208.9 3.0 collective-permute-start.50
  212.1 1.8 collective-permute-done.39
  215.7 15.3 %collective-permute-start.38 = (bf16[2,2,96,768]{3,2,1,0:T(8,128)(2,1)S(1)}, bf16[2,2,96,768]{3,2,1,0:T(8,128)(2,1)S(1)}, u32[]{:S(2)}, u32[]{:S(2)}) collective-permute-start(bf16[2,2,96,768]{3,2,1,0:T(8,128)(2,1)S(1)} %get-tuple-element.102), channel_id=1, source_target_pairs={{0,8},{1,9},{2,10},{3,11},{4,12},{5,13},{6,14},{7,15},{8,0},{9,1},... | collective-permute-start | bytes 1769480 | tf_op jit(solution)/shard_map/ppermute | solution.py:704
  231.0 5.1 %collective-permute-done.46.refs_2_ = bf16[2,4,96,768]{3,2,1,0:T(8,128)(2,1)S(1)} collective-permute-done((bf16[2,4,96,768]{3,2,1,0:T(8,128)(2,1)S(1)}, bf16[2,4,96,768]{3,2,1,0:T(8,128)(2,1)S(1)}, u32[]{:S(2)}, u32[]{:S(2)}) %collective-permute-start.46) | collective-permute-done | bytes 1179680 | tf_op jit(solution)/shard_map/ppermute | solution.py:704
  236.9 16.1 %collective-permute-done.50.refs_6_.refs_7_.refs_8_ = bf16[2,4,96,768]{3,2,1,0:T(8,128)(2,1)S(1)} collective-permute-done((bf16[2,4,96,768]{3,2,1,0:T(8,128)(2,1)S(1)}, bf16[2,4,96,768]{3,2,1,0:T(8,128)(2,1)S(1)}, u32[]{:S(2)}, u32[]{:S(2)}) %collective-permute-start.50) | collective-permute-done | bytes 1179680 | tf_op jit(solution)/shard_map/ppermute | solution.py:704
  254.1 1.6 collective-permute-start.51
  255.8 2.2 collective-permute-start.32
  258.0 6.0 %collective-permute-done.40.refs_6_.refs_7_.refs_8_ = bf16[2,2,96,768]{3,2,1,0:T(8,128)(2,1)S(1)} collective-permute-done((bf16[2,2,96,768]{3,2,1,0:T(8,128)(2,1)S(1)}, bf16[2,2,96,768]{3,2,1,0:T(8,128)(2,1)S(1)}, u32[]{:S(2)}, u32[]{:S(2)}) %collective-permute-start.40) | collective-permute-done | bytes 589856 | tf_op jit(solution)/shard_map/ppermute | solution.py:704
  264.1 6.9 %collective-permute-done.28 = bf16[2,128,768]{2,1,0:T(8,128)(2,1)S(1)} collective-permute-done((bf16[2,128,768]{2,1,0:T(8,128)(2,1)S(1)}, bf16[2,128,768]{2,1,0:T(8,128)(2,1)S(1)}, u32[]{:S(2)}, u32[]{:S(2)}) %collective-permute-start.28) | collective-permute-done | bytes 393248 | tf_op jit(solution)/shard_map/ppermute | solution.py:704
  272.6 2.6 collective-permute-done.47.refs_3_
  280.9 2.1 collective-permute-start.33
  283.0 1.6 collective-permute-start.55
  284.6 2.6 collective-permute-done.55
  287.2 2.6 collective-permute-start.56
  289.8 2.1 collective-permute-done.56
  292.0 9.5 %collective-permute-done.52.refs_4_.refs_9_.refs_10_ = bf16[2,2,96,768]{3,2,1,0:T(8,128)(2,1)S(1)} collective-permute-done((bf16[2,2,96,768]{3,2,1,0:T(8,128)(2,1)S(1)}, bf16[2,2,96,768]{3,2,1,0:T(8,128)(2,1)S(1)}, u32[]{:S(2)}, u32[]{:S(2)}) %collective-permute-start.52) | collective-permute-done | bytes 589856 | tf_op jit(solution)/shard_map/ppermute | solution.py:704
  302.9 7.1 %collective-permute-done.57 = f32[12,768]{1,0:T(8,128)S(1)} collective-permute-done((f32[12,768]{1,0:T(8,128)S(1)}, f32[12,768]{1,0:T(8,128)S(1)}, u32[]{:S(2)}, u32[]{:S(2)}) %collective-permute-start.57) | collective-permute-done | bytes 36896 | tf_op jit(solution)/shard_map/ppermute | solution.py:704
  312.6 2.7 collective-permute-start.43
  315.3 12.0 %collective-permute-done.58 = f32[12,768]{1,0:T(8,128)S(1)} collective-permute-done((f32[12,768]{1,0:T(8,128)S(1)}, f32[12,768]{1,0:T(8,128)S(1)}, u32[]{:S(2)}, u32[]{:S(2)}) %collective-permute-start.58) | collective-permute-done | bytes 36896 | tf_op jit(solution)/shard_map/ppermute | solution.py:704
  328.0 1.8 shard_map.363
  329.8 1.7 collective-permute-done.43.refs_5_.refs_11_
  331.5 3.5 %shard_map.366 = (f32[3,96,192]{2,1,0:T(8,128)}, f32[3,96,192]{2,1,0:T(8,128)}, f32[3,96,192]{2,1,0:T(8,128)}, f32[3,96,192]{2,1,0:T(8,128)}, f32[192,96]{1,0:T(...) custom-call(s32[4]{0:T(128)S(1)} %fusion.1.refs_0_.place, ...), custom_call_target="tpu_custom_call" | custom-call | bytes 2359296 | tf_op jit(solution)/shard_map/pallas_call | solution.py:151
  335.0 3.7 %shard_map.369 = (f32[96,768]{1,0:T(8,128)}, f32[96,768]{1,0:T(8,128)}, f32[96,768]{1,0:T(8,128)}, f32[96,768]{1,0:T(8,128)}, f32[96,768]{1,0:T(8,128)}, /*index...) custom-call(s32[4]{0:T(128)S(1)} %fusion.1.refs_0_.place, ...), custom_call_target="tpu_custom_call" | custom-call | bytes 4718592 | tf_op jit(solution)/shard_map/pallas_call | solution.py:151
  (219 shorter events, 49.3 us)
Async XLA Ops:
  2.8 13.2 %collective-permute-start.3 = (bf16[1,4,96,192]{3,2,1,0:T(8,128)(2,1)S(1)}, bf16[1,4,96,192]{3,2,1,0:T(8,128)(2,1)S(1)}, u32[]{:S(2)}, u32[]{:S(2)}) collective-permute-start(bf16[1,4,96,192]{3,2,1,0:T(8,128)(2,1)S(1)} %maximum_bitcast_fusion.1), channel_id=1, source_target_pairs={{0,2},{1,3},{2,0},{3,1},{4,6},{5,7},{6,4},{7,5},{8,10},{9,11},{10,... | collective-permute-start | bytes 442376 | tf_op jit(solution)/shard_map/ppermute | solution.py:704
  16.1 19.1 %collective-permute-start.4 = (bf16[2,4,96,192]{3,2,1,0:T(8,128)(2,1)S(1)}, bf16[2,4,96,192]{3,2,1,0:T(8,128)(2,1)S(1)}, u32[]{:S(2)}, u32[]{:S(2)}) collective-permute-start(bf16[2,4,96,192]{3,2,1,0:T(8,128)(2,1)S(1)} %pad_maximum_fusion.12), channel_id=1, source_target_pairs={{0,1},{1,0},{2,3},{3,2},{4,5},{5,4},{6,7},{7,6},{8,9},{9,8},{10,11... | collective-permute-start | bytes 884744 | tf_op jit(solution)/shard_map/ppermute | solution.py:704
  16.9 20.2 %collective-permute-start.17 = (bf16[1,2,96,768]{3,2,0,1:T(8,128)(2,1)S(1)}, bf16[1,2,96,768]{3,2,0,1:T(8,128)(2,1)S(1)}, u32[]{:S(2)}, u32[]{:S(2)}) collective-permute-start(bf16[1,2,96,768]{3,2,0,1:T(8,128)(2,1)S(1)} %maximum_bitcast_fusion), channel_id=1, source_target_pairs={{0,2},{1,3},{2,0},{3,1},{4,6},{5,7},{6,4},{7,5},{8,10},{9,11},{10,... | collective-permute-start | bytes 884744 | tf_op jit(solution)/shard_map/ppermute | solution.py:704
  20.4 30.1 %collective-permute-start = (bf16[4,128,768]{2,1,0:T(8,128)(2,1)}, bf16[4,128,768]{2,1,0:T(8,128)(2,1)}, u32[]{:S(2)}, u32[]{:S(2)}) collective-permute-start(bf16[4,128,768]{2,1,0:T(8,128)(2,1)} %param.19), channel_id=1, source_target_pairs={{0,0},{1,1},{2,2},{3,3},{4,8},{5,9},{6,10},{7,11},{8,4},{9,5},{10,... | collective-permute-start | bytes 2359304 | tf_op jit(solution)/shard_map/ppermute | solution.py:704
  27.8 22.7 %collective-permute-start.14 = (bf16[4,128,768]{2,1,0:T(8,128)(2,1)}, bf16[4,128,768]{2,1,0:T(8,128)(2,1)}, u32[]{:S(2)}, u32[]{:S(2)}) collective-permute-start(bf16[4,128,768]{2,1,0:T(8,128)(2,1)} %param.20), channel_id=1, source_target_pairs={{0,0},{1,1},{2,2},{3,3},{4,8},{5,9},{6,10},{7,11},{8,4},{9,5},{10,... | collective-permute-start | bytes 2359304 | tf_op jit(solution)/shard_map/ppermute | solution.py:704
  35.5 13.2 %collective-permute-start.5 = (bf16[1,2,96,768]{3,2,1,0:T(8,128)(2,1)S(1)}, bf16[1,2,96,768]{3,2,1,0:T(8,128)(2,1)S(1)}, u32[]{:S(2)}, u32[]{:S(2)}) collective-permute-start(bf16[1,2,96,768]{3,2,1,0:T(8,128)(2,1)S(1)} %get-tuple-element.149), channel_id=1, source_target_pairs={{0,4},{1,5},{2,6},{3,7},{4,0},{5,1},{6,2},{7,3},{8,12},{9,13},{10,... | collective-permute-start | bytes 884744 | tf_op jit(solution)/shard_map/ppermute | solution.py:704
  35.6 14.7 %collective-permute-start.9 = (bf16[1,2,96,768]{3,2,1,0:T(8,128)(2,1)S(1)}, bf16[1,2,96,768]{3,2,1,0:T(8,128)(2,1)S(1)}, u32[]{:S(2)}, u32[]{:S(2)}) collective-permute-start(bf16[1,2,96,768]{3,2,1,0:T(8,128)(2,1)S(1)} %get-tuple-element.148), channel_id=1, source_target_pairs={{0,16},{1,17},{2,18},{3,19},{4,20},{5,21},{6,22},{7,23},{8,24},{9,... | collective-permute-start | bytes 884744 | tf_op jit(solution)/shard_map/ppermute | solution.py:704
  38.0 15.9 %collective-permute-start.18 = (bf16[2,2,96,768]{3,2,0,1:T(8,128)(2,1)}, bf16[2,2,96,768]{3,2,0,1:T(8,128)(2,1)}, u32[]{:S(2)}, u32[]{:S(2)}) collective-permute-start(bf16[2,2,96,768]{3,2,0,1:T(8,128)(2,1)} %pad_maximum_fusion.9), channel_id=1, source_target_pairs={{0,1},{1,0},{2,3},{3,2},{4,5},{5,4},{6,7},{7,6},{8,9},{9,8},{10,11... | collective-permute-start | bytes 1769480 | tf_op jit(solution)/shard_map/ppermute | solution.py:704
  48.8 26.2 %collective-permute-start.6 = (bf16[2,2,96,768]{3,2,1,0:T(8,128)(2,1)S(1)}, bf16[2,2,96,768]{3,2,1,0:T(8,128)(2,1)S(1)}, u32[]{:S(2)}, u32[]{:S(2)}) collective-permute-start(bf16[2,2,96,768]{3,2,1,0:T(8,128)(2,1)S(1)} %pad_maximum_fusion.7.refs_2_), channel_id=1, source_target_pairs={{0,16},{1,17},{2,18},{3,19},{4,20},{5,21},{6,22},{7,23},{8,24},{9,... | collective-permute-start | bytes 1769480 | tf_op jit(solution)/shard_map/ppermute | solution.py:704
  50.4 27.0 %collective-permute-start.10 = (bf16[2,2,96,768]{3,2,1,0:T(8,128)(2,1)S(1)}, bf16[2,2,96,768]{3,2,1,0:T(8,128)(2,1)S(1)}, u32[]{:S(2)}, u32[]{:S(2)}) collective-permute-start(bf16[2,2,96,768]{3,2,1,0:T(8,128)(2,1)S(1)} %pad_maximum_fusion.8.refs_6_), channel_id=1, source_target_pairs={{0,4},{1,5},{2,6},{3,7},{4,0},{5,1},{6,2},{7,3},{8,12},{9,13},{10,... | collective-permute-start | bytes 1769480 | tf_op jit(solution)/shard_map/ppermute | solution.py:704
  53.8 21.1 %collective-permute-start.1 = (bf16[2,128,768]{2,1,0:T(8,128)(2,1)}, bf16[2,128,768]{2,1,0:T(8,128)(2,1)}, u32[]{:S(2)}, u32[]{:S(2)}) collective-permute-start(bf16[2,128,768]{2,1,0:T(8,128)(2,1)} %pad_maximum_fusion.10), channel_id=1, source_target_pairs={{0,2},{1,3},{2,0},{3,1},{4,6},{5,7},{6,4},{7,5},{8,10},{9,11},{10,... | collective-permute-start | bytes 1179656 | tf_op jit(solution)/shard_map/ppermute | solution.py:704
  56.0 22.7 %collective-permute-start.23 = (bf16[1,4,96,768]{3,2,1,0:T(8,128)(2,1)}, bf16[1,4,96,768]{3,2,1,0:T(8,128)(2,1)}, u32[]{:S(2)}, u32[]{:S(2)}) collective-permute-start(bf16[1,4,96,768]{3,2,1,0:T(8,128)(2,1)} %get-tuple-element.134), channel_id=1, source_target_pairs={{0,16},{1,17},{2,18},{3,19},{4,20},{5,21},{6,22},{7,23},{8,24},{9,... | collective-permute-start | bytes 1769480 | tf_op jit(solution)/shard_map/ppermute | solution.py:704
  56.6 22.4 %collective-permute-start.19 = (bf16[1,4,96,768]{3,2,1,0:T(8,128)(2,1)S(1)}, bf16[1,4,96,768]{3,2,1,0:T(8,128)(2,1)}, u32[]{:S(2)}, u32[]{:S(2)}) collective-permute-start(bf16[1,4,96,768]{3,2,1,0:T(8,128)(2,1)S(1)} %get-tuple-element.135), channel_id=1, source_target_pairs={{0,4},{1,5},{2,6},{3,7},{4,0},{5,1},{6,2},{7,3},{8,12},{9,13},{10,... | collective-permute-start | bytes 1769480 | tf_op jit(solution)/shard_map/ppermute | solution.py:704
  77.4 13.0 %collective-permute-start.2 = (bf16[2,128,768]{2,1,0:T(8,128)(2,1)S(1)}, bf16[2,128,768]{2,1,0:T(8,128)(2,1)S(1)}, u32[]{:S(2)}, u32[]{:S(2)}) collective-permute-start(bf16[2,128,768]{2,1,0:T(8,128)(2,1)S(1)} %pad_maximum_fusion.11), channel_id=1, source_target_pairs={{0,1},{1,0},{2,3},{3,2},{4,5},{5,4},{6,7},{7,6},{8,9},{9,8},{10,11... | collective-permute-start | bytes 1179656 | tf_op jit(solution)/shard_map/ppermute | solution.py:704
  78.7 12.5 %collective-permute-start.8 = (bf16[2,2,96,768]{3,2,1,0:T(8,128)(2,1)S(1)}, bf16[2,2,96,768]{3,2,1,0:T(8,128)(2,1)S(1)}, u32[]{:S(2)}, u32[]{:S(2)}) collective-permute-start(bf16[2,2,96,768]{3,2,1,0:T(8,128)(2,1)S(1)} %collective-permute-done.6.refs_3_), channel_id=1, source_target_pairs={{0,8},{1,9},{2,10},{3,11},{4,12},{5,13},{6,14},{7,15},{8,0},{9,1},... | collective-permute-start | bytes 1769480 | tf_op jit(solution)/shard_map/ppermute | solution.py:704
  79.0 12.3 %collective-permute-start.12 = (bf16[2,2,96,768]{3,2,1,0:T(8,128)(2,1)S(1)}, bf16[2,2,96,768]{3,2,1,0:T(8,128)(2,1)S(1)}, u32[]{:S(2)}, u32[]{:S(2)}) collective-permute-start(bf16[2,2,96,768]{3,2,1,0:T(8,128)(2,1)S(1)} %collective-permute-done.10.refs_7_), channel_id=1, source_target_pairs={{0,8},{1,9},{2,10},{3,11},{4,12},{5,13},{6,14},{7,15},{8,0},{9,1},... | collective-permute-start | bytes 1769480 | tf_op jit(solution)/shard_map/ppermute | solution.py:704
  82.4 20.7 %collective-permute-start.15 = (bf16[2,128,768]{2,1,0:T(8,128)(2,1)S(1)}, bf16[2,128,768]{2,1,0:T(8,128)(2,1)S(1)}, u32[]{:S(2)}, u32[]{:S(2)}) collective-permute-start(bf16[2,128,768]{2,1,0:T(8,128)(2,1)S(1)} %pad_maximum_fusion.13), channel_id=1, source_target_pairs={{0,2},{1,3},{2,0},{3,1},{4,6},{5,7},{6,4},{7,5},{8,10},{9,11},{10,... | collective-permute-start | bytes 1179656 | tf_op jit(solution)/shard_map/ppermute | solution.py:704
  83.6 30.0 %collective-permute-start.20 = (bf16[2,4,96,768]{3,2,1,0:T(8,128)(2,1)S(1)}, bf16[2,4,96,768]{3,2,1,0:T(8,128)(2,1)S(1)}, u32[]{:S(2)}, u32[]{:S(2)}) collective-permute-start(bf16[2,4,96,768]{3,2,1,0:T(8,128)(2,1)S(1)} %pad_maximum_fusion.1.refs_4_), channel_id=1, source_target_pairs={{0,16},{1,17},{2,18},{3,19},{4,20},{5,21},{6,22},{7,23},{8,24},{9,... | collective-permute-start | bytes 3538952 | tf_op jit(solution)/shard_map/ppermute | solution.py:704
  90.4 27.2 %collective-permute-start.24 = (bf16[2,4,96,768]{3,2,1,0:T(8,128)(2,1)S(1)}, bf16[2,4,96,768]{3,2,1,0:T(8,128)(2,1)S(1)}, u32[]{:S(2)}, u32[]{:S(2)}) collective-permute-start(bf16[2,4,96,768]{3,2,1,0:T(8,128)(2,1)S(1)} %pad_maximum_fusion.2.refs_8_), channel_id=1, source_target_pairs={{0,4},{1,5},{2,6},{3,7},{4,0},{5,1},{6,2},{7,3},{8,12},{9,13},{10,... | collective-permute-start | bytes 3538952 | tf_op jit(solution)/shard_map/ppermute | solution.py:704
  95.3 23.9 %collective-permute-start.13 = (bf16[2,512,768]{2,1,0:T(8,128)(2,1)S(1)}, bf16[2,512,768]{2,1,0:T(8,128)(2,1)S(1)}, u32[]{:S(2)}, u32[]{:S(2)}) collective-permute-start(bf16[2,512,768]{2,1,0:T(8,128)(2,1)S(1)} %get-tuple-element.77.own_ref), channel_id=1, source_target_pairs={{0,8},{1,9},{2,10},{3,11},{4,12},{5,13},{6,14},{7,15},{8,0},{9,1},... | collective-permute-start | bytes 4718600 | tf_op jit(solution)/shard_map/ppermute | solution.py:704
  103.2 35.1 %collective-permute-start.21 = (bf16[2,4,96,768]{3,2,1,0:T(8,128)(2,1)S(1)}, bf16[2,4,96,768]{3,2,1,0:T(8,128)(2,1)S(1)}, u32[]{:S(2)}, u32[]{:S(2)}) collective-permute-start(bf16[2,4,96,768]{3,2,1,0:T(8,128)(2,1)S(1)} %pad_maximum_fusion.1.refs_4_), channel_id=1, source_target_pairs={{0,8},{1,9},{2,10},{3,11},{4,12},{5,13},{6,14},{7,15},{8,0},{9,1},... | collective-permute-start | bytes 3538952 | tf_op jit(solution)/shard_map/ppermute | solution.py:704
  113.6 24.7 %collective-permute-start.25 = (bf16[2,4,96,768]{3,2,1,0:T(8,128)(2,1)S(1)}, bf16[2,4,96,768]{3,2,1,0:T(8,128)(2,1)S(1)}, u32[]{:S(2)}, u32[]{:S(2)}) collective-permute-start(bf16[2,4,96,768]{3,2,1,0:T(8,128)(2,1)S(1)} %pad_maximum_fusion.2.refs_8_), channel_id=1, source_target_pairs={{0,8},{1,9},{2,10},{3,11},{4,12},{5,13},{6,14},{7,15},{8,0},{9,1},... | collective-permute-start | bytes 3538952 | tf_op jit(solution)/shard_map/ppermute | solution.py:704
  113.6 24.7 %collective-permute-start.22 = (bf16[2,4,96,768]{3,2,1,0:T(8,128)(2,1)S(1)}, bf16[2,4,96,768]{3,2,1,0:T(8,128)(2,1)S(1)}, u32[]{:S(2)}, u32[]{:S(2)}) collective-permute-start(bf16[2,4,96,768]{3,2,1,0:T(8,128)(2,1)S(1)} %collective-permute-done.20.refs_5_), channel_id=1, source_target_pairs={{0,8},{1,9},{2,10},{3,11},{4,12},{5,13},{6,14},{7,15},{8,0},{9,1},... | collective-permute-start | bytes 3538952 | tf_op jit(solution)/shard_map/ppermute | solution.py:704
  117.6 20.8 %collective-permute-start.26 = (bf16[2,4,96,768]{3,2,1,0:T(8,128)(2,1)S(1)}, bf16[2,4,96,768]{3,2,1,0:T(8,128)(2,1)S(1)}, u32[]{:S(2)}, u32[]{:S(2)}) collective-permute-start(bf16[2,4,96,768]{3,2,1,0:T(8,128)(2,1)S(1)} %collective-permute-done.24.refs_9_), channel_id=1, source_target_pairs={{0,8},{1,9},{2,10},{3,11},{4,12},{5,13},{6,14},{7,15},{8,0},{9,1},... | collective-permute-start | bytes 3538952 | tf_op jit(solution)/shard_map/ppermute | solution.py:704
  192.3 15.6 %collective-permute-start.49 = (bf16[2,4,96,768]{3,2,1,0:T(8,128)(2,1)S(1)}, bf16[2,4,96,768]{3,2,1,0:T(8,128)(2,1)S(1)}, u32[]{:S(2)}, u32[]{:S(2)}) collective-permute-start(bf16[2,4,96,768]{3,2,1,0:T(8,128)(2,1)S(1)} %copy-done.35), channel_id=1, source_target_pairs={{0,8},{1,9},{2,10},{3,11},{4,12},{5,13},{6,14},{7,15},{8,0},{9,1},... | collective-permute-start | bytes 3538952 | tf_op jit(solution)/shard_map/ppermute | solution.py:704
  192.8 14.5 %collective-permute-start.27 = (bf16[2,128,768]{2,1,0:T(8,128)(2,1)S(1)}, bf16[2,128,768]{2,1,0:T(8,128)(2,1)S(1)}, u32[]{:S(2)}, u32[]{:S(2)}) collective-permute-start(bf16[2,128,768]{2,1,0:T(8,128)(2,1)S(1)} %bitcast.53), channel_id=1, source_target_pairs={{0,1},{1,0},{2,3},{3,2},{4,5},{5,4},{6,7},{7,6},{8,9},{9,8},{10,11... | collective-permute-start | bytes 1179656 | tf_op jit(solution)/shard_map/ppermute | solution.py:704
  192.8 16.1 %collective-permute-start.44 = (bf16[2,4,96,768]{3,2,1,0:T(8,128)(2,1)S(1)}, bf16[2,4,96,768]{3,2,1,0:T(8,128)(2,1)S(1)}, u32[]{:S(2)}, u32[]{:S(2)}) collective-permute-start(bf16[2,4,96,768]{3,2,1,0:T(8,128)(2,1)S(1)} %get-tuple-element.108), channel_id=1, source_target_pairs={{0,8},{1,9},{2,10},{3,11},{4,12},{5,13},{6,14},{7,15},{8,0},{9,1},... | collective-permute-start | bytes 3538952 | tf_op jit(solution)/shard_map/ppermute | solution.py:704
  195.2 20.4 %collective-permute-start.48 = (bf16[2,4,96,768]{3,2,1,0:T(8,128)(2,1)S(1)}, bf16[2,4,96,768]{3,2,1,0:T(8,128)(2,1)S(1)}, u32[]{:S(2)}, u32[]{:S(2)}) collective-permute-start(bf16[2,4,96,768]{3,2,1,0:T(8,128)(2,1)S(1)} %copy-done.32), channel_id=1, source_target_pairs={{0,8},{1,9},{2,10},{3,11},{4,12},{5,13},{6,14},{7,15},{8,0},{9,1},... | collective-permute-start | bytes 3538952 | tf_op jit(solution)/shard_map/ppermute | solution.py:704
  200.7 11.1 %collective-permute-start.35 = (bf16[2,2,96,768]{3,2,1,0:T(8,128)(2,1)S(1)}, bf16[2,2,96,768]{3,2,1,0:T(8,128)(2,1)S(1)}, u32[]{:S(2)}, u32[]{:S(2)}) collective-permute-start(bf16[2,2,96,768]{3,2,1,0:T(8,128)(2,1)S(1)} %get-tuple-element.100), channel_id=1, source_target_pairs={{0,8},{1,9},{2,10},{3,11},{4,12},{5,13},{6,14},{7,15},{8,0},{9,1},... | collective-permute-start | bytes 1769480 | tf_op jit(solution)/shard_map/ppermute | solution.py:704
  207.2 28.9 %collective-permute-start.46 = (bf16[2,4,96,768]{3,2,1,0:T(8,128)(2,1)S(1)}, bf16[2,4,96,768]{3,2,1,0:T(8,128)(2,1)S(1)}, u32[]{:S(2)}, u32[]{:S(2)}) collective-permute-start(bf16[2,4,96,768]{3,2,1,0:T(8,128)(2,1)S(1)} %add_convert_fusion.1), channel_id=1, source_target_pairs={{0,16},{1,17},{2,18},{3,19},{4,20},{5,21},{6,22},{7,23},{8,24},{9,... | collective-permute-start | bytes 3538952 | tf_op jit(solution)/shard_map/ppermute | solution.py:704
  208.9 44.1 %collective-permute-start.50 = (bf16[2,4,96,768]{3,2,1,0:T(8,128)(2,1)S(1)}, bf16[2,4,96,768]{3,2,1,0:T(8,128)(2,1)S(1)}, u32[]{:S(2)}, u32[]{:S(2)}) collective-permute-start(bf16[2,4,96,768]{3,2,1,0:T(8,128)(2,1)S(1)} %add_convert_fusion), channel_id=1, source_target_pairs={{0,4},{1,5},{2,6},{3,7},{4,0},{5,1},{6,2},{7,3},{8,12},{9,13},{10,... | collective-permute-start | bytes 3538952 | tf_op jit(solution)/shard_map/ppermute | solution.py:704
  213.9 40.1 %collective-permute-start.34 = (bf16[2,2,96,768]{3,2,1,0:T(8,128)(2,1)S(1)}, bf16[2,2,96,768]{3,2,1,0:T(8,128)(2,1)S(1)}, u32[]{:S(2)}, u32[]{:S(2)}) collective-permute-start(bf16[2,2,96,768]{3,2,1,0:T(8,128)(2,1)S(1)} %get-tuple-element.98), channel_id=1, source_target_pairs={{0,8},{1,9},{2,10},{3,11},{4,12},{5,13},{6,14},{7,15},{8,0},{9,1},... | collective-permute-start | bytes 1769480 | tf_op jit(solution)/shard_map/ppermute | solution.py:704
  214.0 40.1 %collective-permute-start.36 = (bf16[2,2,96,768]{3,2,1,0:T(8,128)(2,1)S(1)}, bf16[2,2,96,768]{3,2,1,0:T(8,128)(2,1)S(1)}, u32[]{:S(2)}, u32[]{:S(2)}) collective-permute-start(bf16[2,2,96,768]{3,2,1,0:T(8,128)(2,1)S(1)} %add_convert_fusion.5), channel_id=1, source_target_pairs={{0,16},{1,17},{2,18},{3,19},{4,20},{5,21},{6,22},{7,23},{8,24},{9,... | collective-permute-start | bytes 1769480 | tf_op jit(solution)/shard_map/ppermute | solution.py:704
  215.7 40.1 %collective-permute-start.38 = (bf16[2,2,96,768]{3,2,1,0:T(8,128)(2,1)S(1)}, bf16[2,2,96,768]{3,2,1,0:T(8,128)(2,1)S(1)}, u32[]{:S(2)}, u32[]{:S(2)}) collective-permute-start(bf16[2,2,96,768]{3,2,1,0:T(8,128)(2,1)S(1)} %get-tuple-element.102), channel_id=1, source_target_pairs={{0,8},{1,9},{2,10},{3,11},{4,12},{5,13},{6,14},{7,15},{8,0},{9,1},... | collective-permute-start | bytes 1769480 | tf_op jit(solution)/shard_map/ppermute | solution.py:704
  236.2 27.8 %collective-permute-start.40 = (bf16[2,2,96,768]{3,2,1,0:T(8,128)(2,1)S(1)}, bf16[2,2,96,768]{3,2,1,0:T(8,128)(2,1)S(1)}, u32[]{:S(2)}, u32[]{:S(2)}) collective-permute-start(bf16[2,2,96,768]{3,2,1,0:T(8,128)(2,1)S(1)} %add_convert_fusion.4), channel_id=1, source_target_pairs={{0,4},{1,5},{2,6},{3,7},{4,0},{5,1},{6,2},{7,3},{8,12},{9,13},{10,... | collective-permute-start | bytes 1769480 | tf_op jit(solution)/shard_map/ppermute | solution.py:704
  253.0 18.0 %collective-permute-start.28 = (bf16[2,128,768]{2,1,0:T(8,128)(2,1)S(1)}, bf16[2,128,768]{2,1,0:T(8,128)(2,1)S(1)}, u32[]{:S(2)}, u32[]{:S(2)}) collective-permute-start(bf16[2,128,768]{2,1,0:T(8,128)(2,1)S(1)} %pad_maximum_fusion.15), channel_id=1, source_target_pairs={{0,2},{1,3},{2,0},{3,1},{4,6},{5,7},{6,4},{7,5},{8,10},{9,11},{10,... | collective-permute-start | bytes 1179656 | tf_op jit(solution)/shard_map/ppermute | solution.py:704
  254.0 21.1 %collective-permute-start.47 = (bf16[1,4,96,768]{3,2,1,0:T(8,128)(2,1)S(1)}, bf16[1,4,96,768]{3,2,1,0:T(8,128)(2,1)S(1)}, u32[]{:S(2)}, u32[]{:S(2)}) collective-permute-start(bf16[1,4,96,768]{3,2,1,0:T(8,128)(2,1)S(1)} %add_convert_fusion.3), channel_id=1, source_target_pairs={{0,4},{1,5},{2,6},{3,7},{4,0},{5,1},{6,2},{7,3},{8,12},{9,13},{10,... | collective-permute-start | bytes 1769480 | tf_op jit(solution)/shard_map/ppermute | solution.py:704
  254.1 22.0 %collective-permute-start.51 = (bf16[1,4,96,768]{3,2,1,0:T(8,128)(2,1)S(1)}, bf16[1,4,96,768]{3,2,1,0:T(8,128)(2,1)S(1)}, u32[]{:S(2)}, u32[]{:S(2)}) collective-permute-start(bf16[1,4,96,768]{3,2,1,0:T(8,128)(2,1)S(1)} %add_convert_fusion.2), channel_id=1, source_target_pairs={{0,16},{1,17},{2,18},{3,19},{4,20},{5,21},{6,22},{7,23},{8,24},{9,... | collective-permute-start | bytes 1769480 | tf_op jit(solution)/shard_map/ppermute | solution.py:704
  255.8 25.0 %collective-permute-start.32 = (bf16[2,128,768]{2,1,0:T(8,128)(2,1)S(1)}, bf16[2,128,768]{2,1,0:T(8,128)(2,1)S(1)}, u32[]{:S(2)}, u32[]{:S(2)}) collective-permute-start(bf16[2,128,768]{2,1,0:T(8,128)(2,1)S(1)} %slice.161), channel_id=1, source_target_pairs={{0,1},{1,0},{2,3},{3,2},{4,5},{5,4},{6,7},{7,6},{8,9},{9,8},{10,11... | collective-permute-start | bytes 1179656 | tf_op jit(solution)/shard_map/ppermute | solution.py:704
  264.0 14.3 %collective-permute-start.37 = (bf16[1,2,96,768]{3,2,1,0:T(8,128)(2,1)S(1)}, bf16[1,2,96,768]{3,2,1,0:T(8,128)(2,1)S(1)}, u32[]{:S(2)}, u32[]{:S(2)}) collective-permute-start(bf16[1,2,96,768]{3,2,1,0:T(8,128)(2,1)S(1)} %add_convert_fusion.7), channel_id=1, source_target_pairs={{0,4},{1,5},{2,6},{3,7},{4,0},{5,1},{6,2},{7,3},{8,12},{9,13},{10,... | collective-permute-start | bytes 884744 | tf_op jit(solution)/shard_map/ppermute | solution.py:704
  275.1 35.3 %collective-permute-start.29 = (bf16[4,128,768]{2,1,0:T(8,128)(2,1)S(1)}, bf16[4,128,768]{2,1,0:T(8,128)(2,1)S(1)}, u32[]{:S(2)}, u32[]{:S(2)}) collective-permute-start(bf16[4,128,768]{2,1,0:T(8,128)(2,1)S(1)} %pad_maximum_fusion.5), channel_id=1, source_target_pairs={{0,0},{1,1},{2,2},{3,3},{4,8},{5,9},{6,10},{7,11},{8,4},{9,5},{10,... | collective-permute-start | bytes 2359304 | tf_op jit(solution)/shard_map/ppermute | solution.py:704
  277.0 24.5 %collective-permute-start.52 = (bf16[2,2,96,768]{3,2,1,0:T(8,128)(2,1)S(1)}, bf16[2,2,96,768]{3,2,1,0:T(8,128)(2,1)S(1)}, u32[]{:S(2)}, u32[]{:S(2)}) collective-permute-start(bf16[2,2,96,768]{3,2,1,0:T(8,128)(2,1)S(1)} %shard_map.367), channel_id=1, source_target_pairs={{0,1},{1,0},{2,3},{3,2},{4,5},{5,4},{6,7},{7,6},{8,9},{9,8},{10,11... | collective-permute-start | bytes 1769480 | tf_op jit(solution)/shard_map/ppermute | solution.py:704
  280.6 31.3 %collective-permute-start.42 = (bf16[4,96,384]{2,1,0:T(8,128)(2,1)S(1)}, bf16[4,96,384]{2,1,0:T(8,128)(2,1)S(1)}, u32[]{:S(2)}, u32[]{:S(2)}) collective-permute-start(bf16[4,96,384]{2,1,0:T(8,128)(2,1)S(1)} %shard_map.364), channel_id=1, source_target_pairs={{0,1},{1,0},{2,3},{3,2},{4,5},{5,4},{6,7},{7,6},{8,9},{9,8},{10,11... | collective-permute-start | bytes 884744 | tf_op jit(solution)/shard_map/ppermute | solution.py:704
  280.9 47.1 %collective-permute-start.33 = (bf16[2,128,768]{2,1,0:T(8,128)(2,1)S(1)}, bf16[2,128,768]{2,1,0:T(8,128)(2,1)S(1)}, u32[]{:S(2)}, u32[]{:S(2)}) collective-permute-start(bf16[2,128,768]{2,1,0:T(8,128)(2,1)S(1)} %pad_maximum_fusion.16), channel_id=1, source_target_pairs={{0,2},{1,3},{2,0},{3,1},{4,6},{5,7},{6,4},{7,5},{8,10},{9,11},{10,... | collective-permute-start | bytes 1179656 | tf_op jit(solution)/shard_map/ppermute | solution.py:704
  291.9 18.1 %collective-permute-start.57 = (f32[12,768]{1,0:T(8,128)S(1)}, f32[12,768]{1,0:T(8,128)S(1)}, u32[]{:S(2)}, u32[]{:S(2)}) collective-permute-start(f32[12,768]{1,0:T(8,128)S(1)} %add.110), channel_id=1, source_target_pairs={{0,1},{1,0},{2,3},{3,2},{4,5},{5,4},{6,7},{7,6},{8,9},{9,8},{10,11... | collective-permute-start | bytes 110600 | tf_op jit(solution)/shard_map/ppermute | solution.py:704
  302.2 32.8 %collective-permute-start.53 = (bf16[2,1,96,768]{3,2,1,0:T(8,128)(2,1)S(1)}, bf16[2,1,96,768]{3,2,1,0:T(8,128)(2,1)S(1)}, u32[]{:S(2)}, u32[]{:S(2)}) collective-permute-start(bf16[2,1,96,768]{3,2,1,0:T(8,128)(2,1)S(1)} %shard_map.368), channel_id=1, source_target_pairs={{0,2},{1,3},{2,0},{3,1},{4,6},{5,7},{6,4},{7,5},{8,10},{9,11},{10,... | collective-permute-start | bytes 884744 | tf_op jit(solution)/shard_map/ppermute | solution.py:704
  310.0 17.3 %collective-permute-start.58 = (f32[12,768]{1,0:T(8,128)S(1)}, f32[12,768]{1,0:T(8,128)S(1)}, u32[]{:S(2)}, u32[]{:S(2)}) collective-permute-start(f32[12,768]{1,0:T(8,128)S(1)} %add.111), channel_id=1, source_target_pairs={{0,2},{1,3},{2,0},{3,1},{4,6},{5,7},{6,4},{7,5},{8,10},{9,11},{10,... | collective-permute-start | bytes 110600 | tf_op jit(solution)/shard_map/ppermute | solution.py:704
  312.6 18.9 %collective-permute-start.43 = (bf16[4,96,192]{2,1,0:T(8,128)(2,1)S(1)}, bf16[4,96,192]{2,1,0:T(8,128)(2,1)S(1)}, u32[]{:S(2)}, u32[]{:S(2)}) collective-permute-start(bf16[4,96,192]{2,1,0:T(8,128)(2,1)S(1)} %shard_map.365), channel_id=1, source_target_pairs={{0,2},{1,3},{2,0},{3,1},{4,6},{5,7},{6,4},{7,5},{8,10},{9,11},{10,... | collective-permute-start | bytes 442376 | tf_op jit(solution)/shard_map/ppermute | solution.py:704
  (52 other events, 559.0 us)
